TPU v7x, 32 devices: a whole 2x2x4 slice. The times are simulated.
32 devices in a mesh: dp: 8 (over y, x, core), seq: 4 (over z).
Axes of the slice: x: 2, y: 2, z: 4, core: 2. Of those that a mesh axis runs over, the one named last changes fastest.
Arguments:
- block_input: bfloat16 [16, 1024, 768], P('dp', 'seq'), may hold values from -6 to 6
- cotangent: bfloat16 [16, 1024, 768], P('dp', 'seq'), may hold values from -6 to 6
- segments: int32 [16, 1024], P('dp'), may hold values from 0 to 3, never falling along the last dimension, each value on 1 to 800 neighbouring positions
- norm_gain: bfloat16 [768], P(('dp', 'seq')), may hold values from 0.5 to 1.5
- w_in: bfloat16 [768, 3352], P(('dp', 'seq')), may hold values from -0.21875 to 0.21875
- conv_weight: bfloat16 [4, 1792], P(None, ('dp', 'seq')), may hold values from -3 to 3
- conv_bias: bfloat16 [1792], P(('dp', 'seq')), may hold values from -0.5 to 0.5
- dt_bias: float32 [24], replicated, may hold values from -6 to -2
- a_log: float32 [24], replicated, may hold values from 0 to 2.77
- d_skip: float32 [24], replicated, may hold values from 0.5 to 1.5
- gate_gain: bfloat16 [1536], P(('dp', 'seq')), may hold values from 0.5 to 1.5
- w_out: bfloat16 [1536, 768], P(('dp', 'seq')), may hold values from -0.15625 to 0.15625
Outputs:
- result: bfloat16 [16, 1024, 768], P('dp', 'seq')
- grad_x: bfloat16 [16, 1024, 768], P('dp', 'seq')
- grad_norm_gain: float32 [768], P(('dp', 'seq'))
- grad_w_in: float32 [768, 3352], P(('dp', 'seq'))
- grad_conv_weight: float32 [4, 1792], P(None, ('dp', 'seq'))
- grad_conv_bias: float32 [1792], P(('dp', 'seq'))
- grad_dt_bias: float32 [24], replicated
- grad_a_log: float32 [24], replicated
- grad_d_skip: float32 [24], replicated
- grad_gate_gain: float32 [1536], P(('dp', 'seq'))
- grad_w_out: float32 [1536, 768], P(('dp', 'seq'))
Inputs may be any that keep to these rules, and one draw needn't show every extreme that they name: `segments`: along each sequence the numbers start at 0, never fall and rise by one where a new document begins; every document has 1 to 800 tokens, and one document of each sequence has exactly 800.
All inputs are finite; a program needn't handle non-finite values.
Results may differ from a plain program's by a relative error of at most 0.012.
Values may be sent and summed in bfloat16 or wider, within the bound.
A program may use at most 128 MiB of HBM per device.

v0:
```python
from functools import partial

import jax
import jax.numpy as jnp
from jax import lax
from jax.sharding import PartitionSpec as P

EPSILON = 1e-05
CONTRACT_ROWS = (((0,), (0,)), ((), ()))
CONTRACT_COLS = (((1,), (1,)), ((), ()))


def shifted(value, axis, steps):
    count = lax.axis_size(axis)
    initial, last = (max(0, -steps), min(count, count - steps))
    return lax.ppermute(value, axis, [(source, source + steps) for source in range(initial, last)])


def norm_input(tokens_f, gain_f):
    inv = lax.rsqrt(jnp.mean(tokens_f * tokens_f, axis=-1, keepdims=True) + EPSILON)
    return tokens_f * inv * gain_f


def mixer_inputs(xbc_ext, dt_raw, conv_w, conv_b, dt_bias, a_log, tap_mask):
    block_len = dt_raw.shape[0]
    pre = conv_b
    for offset in range(4):
        pre = (
            pre
            + conv_w[offset]
            * xbc_ext[offset : offset + block_len]
            * tap_mask[:, offset : offset + 1]
        )
    activated = jax.nn.silu(pre)
    step_size = jax.nn.softplus(dt_raw + dt_bias)
    cumulated = jnp.cumsum(-jnp.exp(a_log) * step_size, axis=0)
    return (activated, step_size, cumulated)


def mixing_weights(affinity, cumulated, step_size, same_doc):
    cum_heads = cumulated.T
    exponent = jnp.where(same_doc[None], cum_heads[:, :, None] - cum_heads[:, None, :], -1e30)
    return affinity[None] * jnp.exp(exponent) * step_size.T[:, None, :]


def end_weights(cumulated, step_size, end_same, carried_last):
    weight_end = jnp.exp(cumulated[-1] - cumulated) * step_size * end_same[:, None]
    block_decay = jnp.exp(cumulated[-1]) * carried_last
    return (weight_end, block_decay)


def read_scale(read_float, cumulated, carried):
    factor = jnp.exp(cumulated) * carried[:, None]
    return factor[:, :, None] * read_float[:, None, :]


def gate_norm(y_values, z_float, gain_f):
    gated_in = y_values * jax.nn.silu(z_float)
    return (
        gated_in
        * lax.rsqrt(jnp.mean(gated_in * gated_in, axis=-1, keepdims=True) + EPSILON)
        * gain_f
    )


def per_device(
    block_input,
    cotangent,
    segments,
    norm_gain,
    w_in,
    conv_weight,
    conv_bias,
    dt_bias,
    a_log,
    d_skip,
    gate_gain,
    w_out,
):
    micro_count, block_len, model_width = block_input.shape
    all_devices = lax.axis_size(("dp", "seq"))
    seq_devices = lax.axis_size("seq")
    block_start = lax.axis_index("seq") * block_len
    inner_width = gate_gain.shape[0] * all_devices
    head_count = dt_bias.shape[0]
    head_width = inner_width // head_count
    xbc_width = conv_bias.shape[0] * all_devices
    state_width = (xbc_width - inner_width) // 2
    proj_width = w_in.shape[1]
    f32 = jnp.float32
    bf16 = jnp.bfloat16

    def one_batch(front_weights, back_weights, tokens, cot_rows, seg_row):
        w_in_all, gain_all, conv_w_all, conv_b_all = front_weights
        w_out_all, gate_all = back_weights
        tokens_f = tokens.astype(f32)
        normed, norm_back = jax.vjp(norm_input, tokens_f, gain_all.astype(f32))
        normed_b = normed.astype(bf16)
        projected = jnp.dot(normed_b, w_in_all, preferred_element_type=f32).astype(bf16)
        xbc_rows = projected[:, inner_width : inner_width + xbc_width]
        rim_rows = shifted(xbc_rows[block_len - 3 :], "seq", 1)
        padded = jnp.concatenate([jnp.full((3,), -1, jnp.int32), seg_row])
        seg_window = lax.dynamic_slice_in_dim(padded, block_start, block_len + 3)
        seg_local = seg_window[3:]
        tap_mask = jnp.stack(
            [seg_window[offset : offset + block_len] == seg_local for offset in range(4)], axis=1
        ).astype(f32)
        xbc_ext = jnp.concatenate([rim_rows, xbc_rows], axis=0).astype(f32)
        dt_raw = projected[:, inner_width + xbc_width :].astype(f32)
        (activated, step_size, cumulated), mixer_back = jax.vjp(
            partial(mixer_inputs, tap_mask=tap_mask),
            xbc_ext,
            dt_raw,
            conv_w_all.astype(f32),
            conv_b_all.astype(f32),
            dt_bias,
            a_log,
        )
        act_b = activated.astype(bf16)
        x_values = act_b[:, :inner_width].reshape(block_len, head_count, head_width)
        write_rows = act_b[:, inner_width : inner_width + state_width]
        read_rows = act_b[:, inner_width + state_width :]
        prior_segment = seg_window[2]
        positions = lax.iota(jnp.int32, block_len)
        same_doc = (seg_local[:, None] == seg_local[None, :]) & (
            positions[None, :] <= positions[:, None]
        )
        carried = (seg_local == prior_segment).astype(f32)
        end_same = (seg_local == seg_local[-1]).astype(f32)
        affinity = lax.dot_general(read_rows, write_rows, CONTRACT_COLS, preferred_element_type=f32)
        mixing, mixing_back = jax.vjp(
            partial(mixing_weights, same_doc=same_doc), affinity, cumulated, step_size
        )
        mixing_b = mixing.astype(bf16)
        within = jnp.einsum("hts,shp->thp", mixing_b, x_values, preferred_element_type=f32)
        x_float = x_values.astype(f32)
        read_float = read_rows.astype(f32)
        (weight_end, block_decay), end_back = jax.vjp(
            partial(end_weights, end_same=end_same, carried_last=carried[-1]), cumulated, step_size
        )
        weighted_b = (x_float * weight_end[:, :, None]).astype(bf16)
        local_state = jnp.einsum("shp,sn->hpn", weighted_b, write_rows, preferred_element_type=f32)

        def relay_state(repeat, incoming):
            return shifted(
                (block_decay[:, None, None] * incoming + local_state).astype(jnp.bfloat16), "seq", 1
            ).astype(jnp.float32)

        state_in = lax.fori_loop(0, seq_devices - 1, relay_state, jnp.zeros_like(local_state))
        state_b = state_in.astype(bf16)
        scaled, scale_back = jax.vjp(partial(read_scale, carried=carried), read_float, cumulated)
        scaled_b = scaled.astype(bf16)
        from_state = jnp.einsum("thn,hpn->thp", scaled_b, state_b, preferred_element_type=f32)
        y_heads = within + from_state + d_skip[None, :, None] * x_float
        z_float = projected[:, :inner_width].astype(f32)
        gated, gate_back = jax.vjp(
            gate_norm, y_heads.reshape(block_len, inner_width), z_float, gate_all.astype(f32)
        )
        gated_b = gated.astype(bf16)
        mixed = jnp.dot(gated_b, w_out_all, preferred_element_type=f32)
        result_rows = (tokens_f + mixed).astype(bf16)
        cot_f = cot_rows.astype(f32)
        grad_wout = lax.dot_general(gated_b, cot_rows, CONTRACT_ROWS, preferred_element_type=f32)
        d_gated = lax.dot_general(cot_rows, w_out_all, CONTRACT_COLS, preferred_element_type=f32)
        grad_y, grad_z, grad_gate = gate_back(d_gated)
        dy_b = grad_y.astype(bf16).reshape(block_len, head_count, head_width)
        dy_float = dy_b.astype(f32)
        grad_skip = jnp.sum(dy_float * x_float, axis=(0, 2))
        d_mixing = jnp.einsum("thp,shp->hts", dy_b, x_values, preferred_element_type=f32)
        dx_within = jnp.einsum("hts,thp->shp", mixing_b, dy_b, preferred_element_type=f32)
        d_affinity, d_cum_mix, d_step_mix = mixing_back(d_mixing)
        state_grad = jnp.einsum("thn,thp->hpn", scaled_b, dy_b, preferred_element_type=f32)
        d_scaled = jnp.einsum("thp,hpn->thn", dy_b, state_b, preferred_element_type=f32)
        d_read_state, d_cum_state = scale_back(d_scaled)

        def relay_grad(repeat, outgoing):
            return shifted(
                (block_decay[:, None, None] * outgoing + state_grad).astype(jnp.bfloat16), "seq", -1
            ).astype(jnp.float32)

        adjoint = lax.fori_loop(0, seq_devices - 1, relay_grad, jnp.zeros_like(state_grad))
        d_decay = jnp.sum(adjoint * state_in, axis=(1, 2))
        adjoint_b = adjoint.astype(bf16)
        d_weighted = jnp.einsum("hpn,sn->shp", adjoint_b, write_rows, preferred_element_type=f32)
        dwrite_state = jnp.einsum("shp,hpn->sn", weighted_b, adjoint_b, preferred_element_type=f32)
        dx_state = d_weighted * weight_end[:, :, None]
        d_wend = jnp.sum(d_weighted * x_float, axis=2)
        d_cum_block, d_step_block = end_back((d_wend, d_decay))
        affinity_b = d_affinity.astype(bf16)
        d_read = jnp.dot(affinity_b, write_rows, preferred_element_type=f32) + d_read_state
        d_write = (
            lax.dot_general(affinity_b, read_rows, CONTRACT_ROWS, preferred_element_type=f32)
            + dwrite_state
        )
        dx_total = dx_within + dx_state + d_skip[None, :, None] * dy_float
        d_act = jnp.concatenate([dx_total.reshape(block_len, inner_width), d_write, d_read], axis=1)
        d_ext, d_dtraw, d_convw, d_convb, d_dtbias, d_alog = mixer_back(
            (d_act, d_step_mix + d_step_block, d_cum_mix + d_cum_state + d_cum_block)
        )
        rim_grad = shifted(d_ext[:3], "seq", -1)
        d_xbc = d_ext[3:] + jnp.pad(rim_grad, ((block_len - 3, 0), (0, 0)))
        d_proj = jnp.concatenate([grad_z, d_xbc, d_dtraw], axis=1).astype(bf16)
        grad_win = lax.dot_general(normed_b, d_proj, CONTRACT_ROWS, preferred_element_type=f32)
        d_normed = lax.dot_general(d_proj, w_in_all, CONTRACT_COLS, preferred_element_type=f32)
        dx_norm, grad_gain = norm_back(d_normed)
        grad_rows = (cot_f + dx_norm).astype(bf16)
        grads = (
            grad_win,
            grad_gain,
            d_convw,
            d_convb,
            grad_gate,
            grad_wout,
            d_dtbias,
            d_alog,
            grad_skip,
        )
        return (result_rows, grad_rows, grads)

    def accumulate(totals, inputs):
        front_weights, back_weights = (
            (
                lax.all_gather(w_in, ("dp", "seq"), axis=0, tiled=True),
                lax.all_gather(norm_gain, ("dp", "seq"), axis=0, tiled=True),
                lax.all_gather(conv_weight, ("dp", "seq"), axis=1, tiled=True),
                lax.all_gather(conv_bias, ("dp", "seq"), axis=0, tiled=True),
            ),
            (
                lax.all_gather(w_out, ("dp", "seq"), axis=0, tiled=True),
                lax.all_gather(gate_gain, ("dp", "seq"), axis=0, tiled=True),
            ),
        )
        result_rows, grad_rows, grads = one_batch(
            front_weights, back_weights, inputs[0], inputs[1], inputs[2]
        )
        return (
            tuple((total + extra for total, extra in zip(totals, grads))),
            (result_rows, grad_rows),
        )

    shapes = (
        (model_width, proj_width),
        (model_width,),
        (4, xbc_width),
        (xbc_width,),
        (inner_width,),
        (inner_width, model_width),
        (head_count,),
        (head_count,),
        (head_count,),
    )
    initial = tuple((jnp.zeros(shape_item, f32) for shape_item in shapes))
    totals, (results, grad_input) = lax.scan(
        accumulate, initial, (block_input, cotangent, segments)
    )
    taps_rows = totals[2].T
    scattered = (
        lax.psum_scatter(totals[0], ("dp", "seq"), scatter_dimension=0, tiled=True),
        lax.psum_scatter(totals[1], ("dp", "seq"), scatter_dimension=0, tiled=True),
        lax.psum_scatter(taps_rows, ("dp", "seq"), scatter_dimension=0, tiled=True),
        lax.psum_scatter(totals[3], ("dp", "seq"), scatter_dimension=0, tiled=True),
        lax.psum_scatter(totals[4], ("dp", "seq"), scatter_dimension=0, tiled=True),
        lax.psum_scatter(totals[5], ("dp", "seq"), scatter_dimension=0, tiled=True),
    )
    head_sums = lax.psum((totals[6], totals[7], totals[8]), ("dp", "seq"))
    return (
        results,
        grad_input,
        scattered[1],
        scattered[0],
        scattered[2].T,
        scattered[3],
        head_sums[0],
        head_sums[1],
        head_sums[2],
        scattered[4],
        scattered[5],
    )


def solution(mesh):
    placed = (
        P("dp", "seq", None),
        P("dp", "seq", None),
        P("dp", None),
        P(("dp", "seq")),
        P(("dp", "seq"), None),
        P(None, ("dp", "seq")),
        P(("dp", "seq")),
        P(),
        P(),
        P(),
        P(("dp", "seq")),
        P(("dp", "seq"), None),
    )
    return jax.shard_map(
        per_device,
        mesh=mesh,
        in_specs=placed,
        out_specs=(
            P("dp", "seq", None),
            P("dp", "seq", None),
            P(("dp", "seq")),
            P(("dp", "seq"), None),
            P(None, ("dp", "seq")),
            P(("dp", "seq")),
            P(),
            P(),
            P(),
            P(("dp", "seq")),
            P(("dp", "seq"), None),
        ),
        check_vma=False,
    )
```

profile of v0, /device:TPU:0, one launch (start us, length us, event | category | flops | bytes accessed | tf_op | source)
XLA Modules:
  0.0 909.9 jit_solution(14254264767861638963)
XLA Ops:
  9.3 621.7 %while.77 = (s32[]{:T(128)}, f32[768,3352]{0,1:T(8,128)}, f32[768]{0:T(1024)}, f32[4,1792]{1,0:T(4,128)}, f32[1792]{0:T(1024)}, /*index=5*/f32[1536]{0:T(1024)},...) while((s32[]{:T(128)}, f32[768,3352]{0,1:T(8,128)}, ...), condition=%wide.region_33.34_spmd.clone, body=%wide.region_0.33_spmd.clone.sunk | while | flops 7147931648 | bytes 377469472 | solution.py:253
  18.8 42.5 %all-reduce.26 = (bf16[768]{0:T(1024)(128)(2,1)S(1)}, bf16[1792]{0:T(1024)(128)(2,1)S(1)}, bf16[1536]{0:T(1024)(128)(2,1)S(1)}) all-reduce(bf16[768]{0:T(1024)(128)(2,1)S(1)} %dynamic-update-slice.9, bf16[1792]{0:T(1024)(128)(2,1)S(1)} %dynamic-update-slice.10, ...), channel_id=1, replica_groups=mesh['dp'=8,'seq'=4] {'dp','seq'}, use_global_device_ids=true, to_apply=%add.12 | all-reduce | flops 4096 | bytes 16384 | tf_op jit(solution)/shard_map/while
  61.9 66.8 %all-gather.3 = bf16[32,56,4]{1,2,0:T(4,128)(2,1)S(1)} all-gather(bf16[1,56,4]{1,2,0:T(4,128)(2,1)} %bitcast.345), channel_id=1, replica_groups=mesh['dp'=8,'seq'=4] {'dp','seq'}, dimensions={0}, use_global_device_ids=true | all-gather | bytes 14784 | tf_op jit(solution)/shard_map/while/body/eval_jaxpr/all_gather | solution.py:225
  130.2 4.9 convolution_convert_fusion.2
  154.3 42.4 %while.78 = (s32[]{:T(128)}, f32[24,64,128]{2,1,0:T(8,128)}, f32[24]{0:T(128)S(1)}, f32[24,64,128]{2,1,0:T(8,128)}, s32[]{:T(128)}, /*index=5*/s32[]{:T(128)}) while((s32[]{:T(128)}, f32[24,64,128]{2,1,0:T(8,128)}, f32[24]{0:T(128)S(1)}, f32[24,64,128]{2,1,0:T(8,128)}, s32[]{:T(128)}, /*index=5*/s32[]{:T(128)}) %tuple.164), condition=%wide.region_5.5_spmd.clone, body=%wide.region_4.4_spmd.clone.sunk | while | flops 983043 | bytes 4718807 | solution.py:149
  156.4 5.1 collective-permute-start
  161.5 4.8 collective-permute-done
  170.6 5.1 collective-permute-start
  175.7 4.8 collective-permute-done
  184.8 5.1 collective-permute-start
  213.4 5.5 fusion.203
  220.5 43.6 %while.79 = (s32[]{:T(128)}, f32[24,64,128]{2,1,0:T(8,128)S(1)}, f32[24]{0:T(128)S(1)}, f32[24,64,128]{2,1,0:T(8,128)}, s32[]{:T(128)}, /*index=5*/s32[]{:T(128)}) while((s32[]{:T(128)}, f32[24,64,128]{2,1,0:T(8,128)S(1)}, f32[24]{0:T(128)S(1)}, f32[24,64,128]{2,1,0:T(8,128)}, s32[]{:T(128)}, /*index=5*/s32[]{:T(128)}) %tuple.181), condition=%wide.region_9.9_spmd.clone, body=%wide.region_8.8_spmd.clone.sunk | while | flops 983043 | bytes 4718807 | solution.py:181
  223.8 10.2 %collective-permute-done.1 = bf16[24,64,128]{2,1,0:T(8,128)(2,1)} collective-permute-done((bf16[24,64,128]{2,1,0:T(8,128)(2,1)}, bf16[24,64,128]{2,1,0:T(8,128)(2,1)}, u32[]{:S(2)}, u32[]{:S(2)}) %collective-permute-start.1) | collective-permute-done | bytes 393248 | tf_op jit(solution)/shard_map/while/body/eval_jaxpr/while/body/eval_jaxpr/ppermute | solution.py:16
  238.4 11.1 %collective-permute-done.1 = bf16[24,64,128]{2,1,0:T(8,128)(2,1)} collective-permute-done((bf16[24,64,128]{2,1,0:T(8,128)(2,1)}, bf16[24,64,128]{2,1,0:T(8,128)(2,1)}, u32[]{:S(2)}, u32[]{:S(2)}) %collective-permute-start.1) | collective-permute-done | bytes 393248 | tf_op jit(solution)/shard_map/while/body/eval_jaxpr/while/body/eval_jaxpr/ppermute | solution.py:16
  254.0 9.0 collective-permute-done.1
  325.9 47.8 %all-reduce.26 = (bf16[768]{0:T(1024)(128)(2,1)S(1)}, bf16[1792]{0:T(1024)(128)(2,1)S(1)}, bf16[1536]{0:T(1024)(128)(2,1)S(1)}) all-reduce(bf16[768]{0:T(1024)(128)(2,1)S(1)} %dynamic-update-slice.9, bf16[1792]{0:T(1024)(128)(2,1)S(1)} %dynamic-update-slice.10, ...), channel_id=1, replica_groups=mesh['dp'=8,'seq'=4] {'dp','seq'}, use_global_device_ids=true, to_apply=%add.12 | all-reduce | flops 4096 | bytes 16384 | tf_op jit(solution)/shard_map/while
  374.4 66.8 %all-gather.3 = bf16[32,56,4]{1,2,0:T(4,128)(2,1)S(1)} all-gather(bf16[1,56,4]{1,2,0:T(4,128)(2,1)} %bitcast.345), channel_id=1, replica_groups=mesh['dp'=8,'seq'=4] {'dp','seq'}, dimensions={0}, use_global_device_ids=true | all-gather | bytes 14784 | tf_op jit(solution)/shard_map/while/body/eval_jaxpr/all_gather | solution.py:225
  442.7 4.9 convolution_convert_fusion.2
  467.3 42.4 %while.78 = (s32[]{:T(128)}, f32[24,64,128]{2,1,0:T(8,128)}, f32[24]{0:T(128)S(1)}, f32[24,64,128]{2,1,0:T(8,128)}, s32[]{:T(128)}, /*index=5*/s32[]{:T(128)}) while((s32[]{:T(128)}, f32[24,64,128]{2,1,0:T(8,128)}, f32[24]{0:T(128)S(1)}, f32[24,64,128]{2,1,0:T(8,128)}, s32[]{:T(128)}, /*index=5*/s32[]{:T(128)}) %tuple.164), condition=%wide.region_5.5_spmd.clone, body=%wide.region_4.4_spmd.clone.sunk | while | flops 983043 | bytes 4718807 | solution.py:149
  469.3 5.1 collective-permute-start
  483.5 5.1 collective-permute-start
  497.7 5.1 collective-permute-start
  526.4 5.5 fusion.203
  533.4 42.5 %while.79 = (s32[]{:T(128)}, f32[24,64,128]{2,1,0:T(8,128)S(1)}, f32[24]{0:T(128)S(1)}, f32[24,64,128]{2,1,0:T(8,128)}, s32[]{:T(128)}, /*index=5*/s32[]{:T(128)}) while((s32[]{:T(128)}, f32[24,64,128]{2,1,0:T(8,128)S(1)}, f32[24]{0:T(128)S(1)}, f32[24,64,128]{2,1,0:T(8,128)}, s32[]{:T(128)}, /*index=5*/s32[]{:T(128)}) %tuple.181), condition=%wide.region_9.9_spmd.clone, body=%wide.region_8.8_spmd.clone.sunk | while | flops 983043 | bytes 4718807 | solution.py:181
  536.7 9.7 %collective-permute-done.1 = bf16[24,64,128]{2,1,0:T(8,128)(2,1)} collective-permute-done((bf16[24,64,128]{2,1,0:T(8,128)(2,1)}, bf16[24,64,128]{2,1,0:T(8,128)(2,1)}, u32[]{:S(2)}, u32[]{:S(2)}) %collective-permute-start.1) | collective-permute-done | bytes 393248 | tf_op jit(solution)/shard_map/while/body/eval_jaxpr/while/body/eval_jaxpr/ppermute | solution.py:16
  550.8 10.6 %collective-permute-done.1 = bf16[24,64,128]{2,1,0:T(8,128)(2,1)} collective-permute-done((bf16[24,64,128]{2,1,0:T(8,128)(2,1)}, bf16[24,64,128]{2,1,0:T(8,128)(2,1)}, u32[]{:S(2)}, u32[]{:S(2)}) %collective-permute-start.1) | collective-permute-done | bytes 393248 | tf_op jit(solution)/shard_map/while/body/eval_jaxpr/while/body/eval_jaxpr/ppermute | solution.py:16
  565.9 9.0 collective-permute-done.1
  603.7 5.5 select_add_fusion.17
  631.7 11.3 %copy.97 = f32[768,3352]{1,0:T(8,128)} copy(f32[768,3352]{0,1:T(8,128)} %get-tuple-element.385) | data formatting | bytes 20594688 | tf_op jit(solution)/shard_map/while | solution.py:253
  643.7 49.2 %all-reduce.24 = (f32[768]{0:T(1024)S(1)}, f32[1792,4]{0,1:T(4,128)S(1)}, f32[1792]{0:T(1024)S(1)}, f32[24]{0:T(128)}, f32[24]{0:T(128)}, /*index=5*/f32[24]{0:T(128)}, f32[1536]{0:T(1024)S(1)}) all-reduce(f32[768]{0:T(1024)S(1)} %copy-done.102, f32[1792,4]{0,1:T(4,128)S(1)} %bitcast.330, ...), channel_id=2, replica_groups=mesh['dp'=8,'seq'=4] {'dp','seq'}, use_global_device_ids=true, to_apply=%region_34.35.clone | all-reduce | flops 11336 | bytes 90688
  695.4 59.6 %reduce-scatter.6.cloned.1.call-done = f32[48,768]{1,0:T(8,128)} async-done(((f32[1536,768]{1,0:T(8,128)}), f32[48,768]{1,0:T(8,128)}) %reduce-scatter.6.cloned.1.call-update) | async-done | bytes 147472 | tf_op jit(solution)/shard_map/reduce_scatter | solution.py:263
  755.0 147.8 %reduce-scatter.8.cloned.1.call-done = f32[24,3352]{1,0:T(8,128)} async-done(((f32[768,3352]{1,0:T(8,128)}), f32[24,3352]{1,0:T(8,128)}) %reduce-scatter.8.cloned.1.call-update) | async-done | bytes 321808
  (747 shorter events, 272.8 us)
Async XLA Ops:
  9.3 120.9 %all-gather.7.cloned.1.call-start = ((), (), s32[]{:S(2)}) async-start(), calls=%async_computation.4 | async-start | bytes 5474304 | tf_op jit(solution)/shard_map/while/body/eval_jaxpr/all_gather | solution.py:223
  10.0 193.7 %all-gather.9.cloned.1.call-start = ((), (), s32[]{:S(2)}) async-start(), calls=%async_computation.5 | async-start | bytes 2433024 | tf_op jit(solution)/shard_map/while/body/eval_jaxpr/all_gather | solution.py:229
  13.4 48.5 %copy-start.96 = (f32[256]{0:T(256)}, f32[256]{0:T(256)S(1)}, u32[]{:S(2)}) copy-start(f32[256]{0:T(256)S(1)} %fusion.191) | copy-start | bytes 3076 | tf_op jit(solution)/shard_map/while
  13.4 121.7 %copy-start.61 = (f32[256]{0:T(256)}, f32[256]{0:T(256)S(1)}, u32[]{:S(2)}) copy-start(f32[256]{0:T(256)S(1)} %fusion.192) | copy-start | bytes 3076 | tf_op jit(solution)/shard_map/while
  14.8 123.8 %copy-start.63 = (f32[256]{0:T(256)}, f32[256]{0:T(256)S(1)}, u32[]{:S(2)}) copy-start(f32[256]{0:T(256)S(1)} %get-tuple-element.949) | copy-start | bytes 3076 | tf_op jit(solution)/shard_map/while
  14.8 123.8 %copy-start.94 = (f32[256]{0:T(256)}, f32[256]{0:T(256)S(1)}, u32[]{:S(2)}) copy-start(f32[256]{0:T(256)S(1)} %get-tuple-element.948) | copy-start | bytes 3076 | tf_op jit(solution)/shard_map/while
  136.8 7.6 collective-permute-start.2
  138.4 12.8 %copy-start.68 = (f32[24,256]{1,0:T(8,128)}, f32[24,256]{1,0:T(8,128)S(1)}, u32[]{:S(2)}) copy-start(f32[24,256]{1,0:T(8,128)S(1)} %get-tuple-element.951) | copy-start | bytes 73732 | tf_op jit(solution)/shard_map/while
  156.4 10.0 %collective-permute-start = (bf16[24,64,128]{2,1,0:T(8,128)(2,1)}, bf16[24,64,128]{2,1,0:T(8,128)(2,1)}, u32[]{:S(2)}, u32[]{:S(2)}) collective-permute-start(bf16[24,64,128]{2,1,0:T(8,128)(2,1)} %fusion.214), channel_id=1, source_target_pairs={{0,1},{1,2},{2,3},{4,5},{5,6},{6,7},{8,9},{9,10},{10,11},{12,13},{... | collective-permute-start | bytes 1179656 | tf_op jit(solution)/shard_map/while/body/eval_jaxpr/while/body/eval_jaxpr/ppermute | solution.py:16
  170.6 10.0 %collective-permute-start = (bf16[24,64,128]{2,1,0:T(8,128)(2,1)}, bf16[24,64,128]{2,1,0:T(8,128)(2,1)}, u32[]{:S(2)}, u32[]{:S(2)}) collective-permute-start(bf16[24,64,128]{2,1,0:T(8,128)(2,1)} %fusion.214), channel_id=1, source_target_pairs={{0,1},{1,2},{2,3},{4,5},{5,6},{6,7},{8,9},{9,10},{10,11},{12,13},{... | collective-permute-start | bytes 1179656 | tf_op jit(solution)/shard_map/while/body/eval_jaxpr/while/body/eval_jaxpr/ppermute | solution.py:16
  184.8 10.0 %collective-permute-start = (bf16[24,64,128]{2,1,0:T(8,128)(2,1)}, bf16[24,64,128]{2,1,0:T(8,128)(2,1)}, u32[]{:S(2)}, u32[]{:S(2)}) collective-permute-start(bf16[24,64,128]{2,1,0:T(8,128)(2,1)} %fusion.214), channel_id=1, source_target_pairs={{0,1},{1,2},{2,3},{4,5},{5,6},{6,7},{8,9},{9,10},{10,11},{12,13},{... | collective-permute-start | bytes 1179656 | tf_op jit(solution)/shard_map/while/body/eval_jaxpr/while/body/eval_jaxpr/ppermute | solution.py:16
  222.5 11.5 %collective-permute-start.1 = (bf16[24,64,128]{2,1,0:T(8,128)(2,1)}, bf16[24,64,128]{2,1,0:T(8,128)(2,1)}, u32[]{:S(2)}, u32[]{:S(2)}) collective-permute-start(bf16[24,64,128]{2,1,0:T(8,128)(2,1)} %fusion.215), channel_id=1, source_target_pairs={{1,0},{2,1},{3,2},{5,4},{6,5},{7,6},{9,8},{10,9},{11,10},{13,12},{... | collective-permute-start | bytes 1179656 | tf_op jit(solution)/shard_map/while/body/eval_jaxpr/while/body/eval_jaxpr/ppermute | solution.py:16
  237.1 12.4 %collective-permute-start.1 = (bf16[24,64,128]{2,1,0:T(8,128)(2,1)}, bf16[24,64,128]{2,1,0:T(8,128)(2,1)}, u32[]{:S(2)}, u32[]{:S(2)}) collective-permute-start(bf16[24,64,128]{2,1,0:T(8,128)(2,1)} %fusion.215), channel_id=1, source_target_pairs={{1,0},{2,1},{3,2},{5,4},{6,5},{7,6},{9,8},{10,9},{11,10},{13,12},{... | collective-permute-start | bytes 1179656 | tf_op jit(solution)/shard_map/while/body/eval_jaxpr/while/body/eval_jaxpr/ppermute | solution.py:16
  252.7 10.3 %collective-permute-start.1 = (bf16[24,64,128]{2,1,0:T(8,128)(2,1)}, bf16[24,64,128]{2,1,0:T(8,128)(2,1)}, u32[]{:S(2)}, u32[]{:S(2)}) collective-permute-start(bf16[24,64,128]{2,1,0:T(8,128)(2,1)} %fusion.215), channel_id=1, source_target_pairs={{1,0},{2,1},{3,2},{5,4},{6,5},{7,6},{9,8},{10,9},{11,10},{13,12},{... | collective-permute-start | bytes 1179656 | tf_op jit(solution)/shard_map/while/body/eval_jaxpr/while/body/eval_jaxpr/ppermute | solution.py:16
  290.4 8.6 collective-permute-start.3
  316.7 126.0 %all-gather.7.cloned.1.call-start = ((), (), s32[]{:S(2)}) async-start(), calls=%async_computation.4 | async-start | bytes 5474304 | tf_op jit(solution)/shard_map/while/body/eval_jaxpr/all_gather | solution.py:223
  317.4 199.3 %all-gather.9.cloned.1.call-start = ((), (), s32[]{:S(2)}) async-start(), calls=%async_computation.5 | async-start | bytes 2433024 | tf_op jit(solution)/shard_map/while/body/eval_jaxpr/all_gather | solution.py:229
  320.6 53.8 %copy-start.96 = (f32[256]{0:T(256)}, f32[256]{0:T(256)S(1)}, u32[]{:S(2)}) copy-start(f32[256]{0:T(256)S(1)} %fusion.191) | copy-start | bytes 3076 | tf_op jit(solution)/shard_map/while
  320.6 127.0 %copy-start.61 = (f32[256]{0:T(256)}, f32[256]{0:T(256)S(1)}, u32[]{:S(2)}) copy-start(f32[256]{0:T(256)S(1)} %fusion.192) | copy-start | bytes 3076 | tf_op jit(solution)/shard_map/while
  322.0 129.0 %copy-start.63 = (f32[256]{0:T(256)}, f32[256]{0:T(256)S(1)}, u32[]{:S(2)}) copy-start(f32[256]{0:T(256)S(1)} %get-tuple-element.949) | copy-start | bytes 3076 | tf_op jit(solution)/shard_map/while
  322.0 129.0 %copy-start.94 = (f32[256]{0:T(256)}, f32[256]{0:T(256)S(1)}, u32[]{:S(2)}) copy-start(f32[256]{0:T(256)S(1)} %get-tuple-element.948) | copy-start | bytes 3076 | tf_op jit(solution)/shard_map/while
  449.3 8.1 collective-permute-start.2
  450.8 13.3 %copy-start.68 = (f32[24,256]{1,0:T(8,128)}, f32[24,256]{1,0:T(8,128)S(1)}, u32[]{:S(2)}) copy-start(f32[24,256]{1,0:T(8,128)S(1)} %get-tuple-element.951) | copy-start | bytes 73732 | tf_op jit(solution)/shard_map/while
  469.3 10.0 %collective-permute-start = (bf16[24,64,128]{2,1,0:T(8,128)(2,1)}, bf16[24,64,128]{2,1,0:T(8,128)(2,1)}, u32[]{:S(2)}, u32[]{:S(2)}) collective-permute-start(bf16[24,64,128]{2,1,0:T(8,128)(2,1)} %fusion.214), channel_id=1, source_target_pairs={{0,1},{1,2},{2,3},{4,5},{5,6},{6,7},{8,9},{9,10},{10,11},{12,13},{... | collective-permute-start | bytes 1179656 | tf_op jit(solution)/shard_map/while/body/eval_jaxpr/while/body/eval_jaxpr/ppermute | solution.py:16
  483.5 10.0 %collective-permute-start = (bf16[24,64,128]{2,1,0:T(8,128)(2,1)}, bf16[24,64,128]{2,1,0:T(8,128)(2,1)}, u32[]{:S(2)}, u32[]{:S(2)}) collective-permute-start(bf16[24,64,128]{2,1,0:T(8,128)(2,1)} %fusion.214), channel_id=1, source_target_pairs={{0,1},{1,2},{2,3},{4,5},{5,6},{6,7},{8,9},{9,10},{10,11},{12,13},{... | collective-permute-start | bytes 1179656 | tf_op jit(solution)/shard_map/while/body/eval_jaxpr/while/body/eval_jaxpr/ppermute | solution.py:16
  497.7 10.0 %collective-permute-start = (bf16[24,64,128]{2,1,0:T(8,128)(2,1)}, bf16[24,64,128]{2,1,0:T(8,128)(2,1)}, u32[]{:S(2)}, u32[]{:S(2)}) collective-permute-start(bf16[24,64,128]{2,1,0:T(8,128)(2,1)} %fusion.214), channel_id=1, source_target_pairs={{0,1},{1,2},{2,3},{4,5},{5,6},{6,7},{8,9},{9,10},{10,11},{12,13},{... | collective-permute-start | bytes 1179656 | tf_op jit(solution)/shard_map/while/body/eval_jaxpr/while/body/eval_jaxpr/ppermute | solution.py:16
  535.5 11.0 %collective-permute-start.1 = (bf16[24,64,128]{2,1,0:T(8,128)(2,1)}, bf16[24,64,128]{2,1,0:T(8,128)(2,1)}, u32[]{:S(2)}, u32[]{:S(2)}) collective-permute-start(bf16[24,64,128]{2,1,0:T(8,128)(2,1)} %fusion.215), channel_id=1, source_target_pairs={{1,0},{2,1},{3,2},{5,4},{6,5},{7,6},{9,8},{10,9},{11,10},{13,12},{... | collective-permute-start | bytes 1179656 | tf_op jit(solution)/shard_map/while/body/eval_jaxpr/while/body/eval_jaxpr/ppermute | solution.py:16
  549.6 11.9 %collective-permute-start.1 = (bf16[24,64,128]{2,1,0:T(8,128)(2,1)}, bf16[24,64,128]{2,1,0:T(8,128)(2,1)}, u32[]{:S(2)}, u32[]{:S(2)}) collective-permute-start(bf16[24,64,128]{2,1,0:T(8,128)(2,1)} %fusion.215), channel_id=1, source_target_pairs={{1,0},{2,1},{3,2},{5,4},{6,5},{7,6},{9,8},{10,9},{11,10},{13,12},{... | collective-permute-start | bytes 1179656 | tf_op jit(solution)/shard_map/while/body/eval_jaxpr/while/body/eval_jaxpr/ppermute | solution.py:16
  564.6 10.3 %collective-permute-start.1 = (bf16[24,64,128]{2,1,0:T(8,128)(2,1)}, bf16[24,64,128]{2,1,0:T(8,128)(2,1)}, u32[]{:S(2)}, u32[]{:S(2)}) collective-permute-start(bf16[24,64,128]{2,1,0:T(8,128)(2,1)} %fusion.215), channel_id=1, source_target_pairs={{1,0},{2,1},{3,2},{5,4},{6,5},{7,6},{9,8},{10,9},{11,10},{13,12},{... | collective-permute-start | bytes 1179656 | tf_op jit(solution)/shard_map/while/body/eval_jaxpr/while/body/eval_jaxpr/ppermute | solution.py:16
  602.3 11.1 %collective-permute-start.3 = (f32[3,1792]{1,0:T(4,128)}, f32[3,1792]{1,0:T(4,128)}, u32[]{:S(2)}, u32[]{:S(2)}) collective-permute-start(f32[3,1792]{1,0:T(4,128)} %copy.152), channel_id=1, source_target_pairs={{1,0},{2,1},{3,2},{5,4},{6,5},{7,6},{9,8},{10,9},{11,10},{13,12},{... | collective-permute-start | bytes 64520 | tf_op jit(solution)/shard_map/while/body/eval_jaxpr/ppermute | solution.py:16
  631.0 123.9 %reduce-scatter.6.cloned.1.call-start = ((), (), s32[]{:S(2)}) async-start(), calls=%async_computation.2 | async-start | bytes 4866048 | tf_op jit(solution)/shard_map/reduce_scatter | solution.py:263
  631.6 271.2 %reduce-scatter.8.cloned.1.call-start = ((), (), s32[]{:S(2)}) async-start(), calls=%async_computation.3 | async-start | bytes 10948608
  (229 other events, 1006.2 us)
Sparse Core Ops, SparseCore 0:
  12.9 68.5 all-gather.6
  84.3 55.5 all-gather.8
  320.3 74.3 all-gather.6
  397.4 55.7 all-gather.8
Sparse Core Ops, SparseCore 1:
  637.6 117.4 reduce-scatter.5
  761.5 141.2 reduce-scatter.7
where the time goes:
time: 913 us; the launch traced here: 910 us
  waiting for transfers between devices  308 us (34%)
  blocking collectives  273 us (30%)
  other arithmetic  128 us (14%)
  matrix products  89.8 us (10%)
  local copies, waits for them, and re-layouts  48.2 us (5%)
  starting transfers between devices  44.1 us (5%)
  between operations  15.3 us (2%)
    unnamed x3, waiting for transfers between devices  148 us
    all_gather x2, blocking collectives, accumulate(): lax.all_gather(conv_weight, ('dp', 'seq'), axis=1, tiled=True)  134 us
    ppermute x16, waiting for transfers between devices, shifted(): lax.ppermute(value, axis, [(source, source + steps) for source in range(i...  97.6 us
    while x2, blocking collectives  90.3 us
    reduce_scatter x1, waiting for transfers between devices, per_device(): lax.psum_scatter(totals[5], ('dp', 'seq'), scatter_dimension=0, tiled=True)  59.6 us
    unnamed x1, blocking collectives  49.2 us
    ppermute x16, starting transfers between devices, shifted(): lax.ppermute(value, axis, [(source, source + steps) for source in range(i...  43.9 us
    while x476, local copies, waits for them, and re-layouts  18.6 us
  transfers between devices with their start and end apart: 22, of which 16 were waited for; matrix products, arithmetic and copies ran while one was open for 13% of the time, Pallas kernels for 0%

commit v1 on v0

v1 whole, which is shorter than its diff:
```python
from functools import partial

import jax
import jax.numpy as jnp
from jax import lax
from jax.sharding import PartitionSpec as P

EPSILON = 1e-05
CONTRACT_ROWS = (((0,), (0,)), ((), ()))
CONTRACT_COLS = (((1,), (1,)), ((), ()))


def hop(value, axis, source, target):
    return lax.ppermute(value, axis, [(source, target)])


def shifted(value, axis, steps):
    count = lax.axis_size(axis)
    initial, last = (max(0, -steps), min(count, count - steps))
    return lax.ppermute(value, axis, [(source, source + steps) for source in range(initial, last)])


def norm_input(tokens_f, gain_f):
    inv = lax.rsqrt(jnp.mean(tokens_f * tokens_f, axis=-1, keepdims=True) + EPSILON)
    return tokens_f * inv * gain_f


def mixer_inputs(xbc_ext, dt_raw, conv_w, conv_b, dt_bias, a_log, tap_mask):
    block_len = dt_raw.shape[1]
    pre = conv_b
    for offset in range(4):
        pre = (
            pre
            + conv_w[offset]
            * xbc_ext[:, offset : offset + block_len]
            * tap_mask[:, :, offset : offset + 1]
        )
    activated = jax.nn.silu(pre)
    step_size = jax.nn.softplus(dt_raw + dt_bias)
    cumulated = jnp.cumsum(-jnp.exp(a_log) * step_size, axis=1)
    return (activated, step_size, cumulated)


def mixing_weights(affinity, cumulated, step_size, same_doc):
    cum_heads = jnp.swapaxes(cumulated, 1, 2)
    exponent = jnp.where(
        same_doc[:, None], cum_heads[:, :, :, None] - cum_heads[:, :, None, :], -1e30
    )
    return affinity[:, None] * jnp.exp(exponent) * jnp.swapaxes(step_size, 1, 2)[:, :, None, :]


def end_weights(cumulated, step_size, end_same, carried_last):
    weight_end = jnp.exp(cumulated[:, -1:] - cumulated) * step_size * end_same[:, :, None]
    block_decay = jnp.exp(cumulated[:, -1]) * carried_last[:, None]
    return (weight_end, block_decay)


def read_scale(read_float, cumulated, carried):
    factor = jnp.exp(cumulated) * carried[:, :, None]
    return factor[:, :, :, None] * read_float[:, :, None, :]


def gate_norm(y_values, z_float, gain_f):
    gated_in = y_values * jax.nn.silu(z_float)
    return (
        gated_in
        * lax.rsqrt(jnp.mean(gated_in * gated_in, axis=-1, keepdims=True) + EPSILON)
        * gain_f
    )


def relay(decay, local, direction):
    count = lax.axis_size("seq")
    chains = []
    for index in range(local.shape[0]):
        incoming = jnp.zeros_like(local[index])
        for step in range(count - 1):
            source = step if direction > 0 else count - 1 - step
            outgoing = decay[index][:, None, None] * incoming + local[index]
            arrived = hop(outgoing.astype(jnp.bfloat16), "seq", source, source + direction)
            incoming = incoming + arrived.astype(jnp.float32)
        chains.append(incoming)
    return jnp.stack(chains)


def per_device(
    block_input,
    cotangent,
    segments,
    norm_gain,
    w_in,
    conv_weight,
    conv_bias,
    dt_bias,
    a_log,
    d_skip,
    gate_gain,
    w_out,
):
    batch, block_len, model_width = block_input.shape
    axes = ("dp", "seq")
    all_devices = lax.axis_size(axes)
    block_start = lax.axis_index("seq") * block_len
    inner_width = gate_gain.shape[0] * all_devices
    head_count = dt_bias.shape[0]
    head_width = inner_width // head_count
    xbc_width = conv_bias.shape[0] * all_devices
    state_width = (xbc_width - inner_width) // 2
    proj_width = w_in.shape[1]
    slab_rows = w_in.shape[0]
    f32 = jnp.float32
    bf16 = jnp.bfloat16

    small_sizes = (norm_gain.size, conv_weight.size, conv_bias.size, gate_gain.size)
    small_cols = -(-sum(small_sizes) // slab_rows)
    smalls = jnp.concatenate(
        [norm_gain, conv_weight.reshape(-1), conv_bias, gate_gain,
         jnp.zeros((small_cols * slab_rows - sum(small_sizes),), bf16)]
    ).reshape(slab_rows, small_cols)
    w_in_full = lax.all_gather(
        jnp.concatenate([w_in, smalls], axis=1), axes, axis=0, tiled=True
    )
    w_out_all = lax.all_gather(w_out, axes, axis=0, tiled=True)
    w_in_all = w_in_full[:, :proj_width]
    small_all = w_in_full[:, proj_width:].reshape(all_devices, slab_rows * small_cols)
    bounds = [0]
    for size in small_sizes:
        bounds.append(bounds[-1] + size)
    gain_all = small_all[:, bounds[0] : bounds[1]].reshape(-1).astype(f32)
    conv_w_all = (
        small_all[:, bounds[1] : bounds[2]]
        .reshape(all_devices, 4, -1)
        .swapaxes(0, 1)
        .reshape(4, xbc_width)
        .astype(f32)
    )
    conv_b_all = small_all[:, bounds[2] : bounds[3]].reshape(-1).astype(f32)
    gate_all = small_all[:, bounds[3] : bounds[4]].reshape(-1).astype(f32)

    tokens_f = block_input.astype(f32)
    normed, norm_back = jax.vjp(norm_input, tokens_f, gain_all)
    normed_b = normed.astype(bf16)
    projected = lax.dot_general(
        normed_b, w_in_all, (((2,), (0,)), ((), ())), preferred_element_type=f32
    ).astype(bf16)
    xbc_rows = projected[:, :, inner_width : inner_width + xbc_width]
    rim_rows = shifted(xbc_rows[:, block_len - 3 :], "seq", 1)
    padded = jnp.concatenate([jnp.full((batch, 3), -1, jnp.int32), segments], axis=1)
    seg_window = lax.dynamic_slice_in_dim(padded, block_start, block_len + 3, axis=1)
    seg_local = seg_window[:, 3:]
    tap_mask = jnp.stack(
        [seg_window[:, offset : offset + block_len] == seg_local for offset in range(4)], axis=2
    ).astype(f32)
    xbc_ext = jnp.concatenate([rim_rows, xbc_rows], axis=1).astype(f32)
    dt_raw = projected[:, :, inner_width + xbc_width :].astype(f32)
    (activated, step_size, cumulated), mixer_back = jax.vjp(
        partial(mixer_inputs, tap_mask=tap_mask),
        xbc_ext,
        dt_raw,
        conv_w_all,
        conv_b_all,
        dt_bias,
        a_log,
    )
    act_b = activated.astype(bf16)
    x_values = act_b[:, :, :inner_width].reshape(batch, block_len, head_count, head_width)
    write_rows = act_b[:, :, inner_width : inner_width + state_width]
    read_rows = act_b[:, :, inner_width + state_width :]
    prior_segment = seg_window[:, 2:3]
    positions = lax.iota(jnp.int32, block_len)
    same_doc = (seg_local[:, :, None] == seg_local[:, None, :]) & (
        positions[None, :] <= positions[:, None]
    )
    carried = (seg_local == prior_segment).astype(f32)
    end_same = (seg_local == seg_local[:, -1:]).astype(f32)
    x_float = x_values.astype(f32)
    read_float = read_rows.astype(f32)
    (weight_end, block_decay), end_back = jax.vjp(
        partial(end_weights, end_same=end_same, carried_last=carried[:, -1]), cumulated, step_size
    )
    weighted_b = (x_float * weight_end[..., None]).astype(bf16)
    local_state = jnp.einsum("bshp,bsn->bhpn", weighted_b, write_rows, preferred_element_type=f32)
    state_in = relay(block_decay, local_state, 1)
    state_b = state_in.astype(bf16)
    affinity = jnp.einsum("btn,bsn->bts", read_rows, write_rows, preferred_element_type=f32)
    mixing, mixing_back = jax.vjp(
        partial(mixing_weights, same_doc=same_doc), affinity, cumulated, step_size
    )
    mixing_b = mixing.astype(bf16)
    within = jnp.einsum("bhts,bshp->bthp", mixing_b, x_values, preferred_element_type=f32)
    scaled, scale_back = jax.vjp(partial(read_scale, carried=carried), read_float, cumulated)
    scaled_b = scaled.astype(bf16)
    from_state = jnp.einsum("bthn,bhpn->bthp", scaled_b, state_b, preferred_element_type=f32)
    y_heads = within + from_state + d_skip[:, None] * x_float
    z_float = projected[:, :, :inner_width].astype(f32)
    gated, gate_back = jax.vjp(
        gate_norm, y_heads.reshape(batch, block_len, inner_width), z_float, gate_all
    )
    gated_b = gated.astype(bf16)
    mixed = lax.dot_general(
        gated_b, w_out_all, (((2,), (0,)), ((), ())), preferred_element_type=f32
    )
    result_rows = (tokens_f + mixed).astype(bf16)
    cot_f = cotangent.astype(f32)
    grad_wout = lax.dot_general(
        gated_b, cotangent, (((0, 1), (0, 1)), ((), ())), preferred_element_type=f32
    ).astype(bf16)
    grad_wout = lax.psum_scatter(grad_wout, axes, scatter_dimension=0, tiled=True).astype(f32)
    d_gated = lax.dot_general(
        cotangent, w_out_all, (((2,), (1,)), ((), ())), preferred_element_type=f32
    )
    grad_y, grad_z, grad_gate = gate_back(d_gated)
    dy_b = grad_y.astype(bf16).reshape(batch, block_len, head_count, head_width)
    dy_float = dy_b.astype(f32)
    state_grad = jnp.einsum("bthn,bthp->bhpn", scaled_b, dy_b, preferred_element_type=f32)
    adjoint = relay(block_decay, state_grad, -1)
    grad_skip = jnp.sum(dy_float * x_float, axis=(0, 1, 3))
    d_mixing = jnp.einsum("bthp,bshp->bhts", dy_b, x_values, preferred_element_type=f32)
    dx_within = jnp.einsum("bhts,bthp->bshp", mixing_b, dy_b, preferred_element_type=f32)
    d_affinity, d_cum_mix, d_step_mix = mixing_back(d_mixing)
    d_scaled = jnp.einsum("bthp,bhpn->bthn", dy_b, state_b, preferred_element_type=f32)
    d_read_state, d_cum_state = scale_back(d_scaled)
    d_decay = jnp.sum(adjoint * state_in, axis=(2, 3))
    adjoint_b = adjoint.astype(bf16)
    d_weighted = jnp.einsum("bhpn,bsn->bshp", adjoint_b, write_rows, preferred_element_type=f32)
    dwrite_state = jnp.einsum("bshp,bhpn->bsn", weighted_b, adjoint_b, preferred_element_type=f32)
    dx_state = d_weighted * weight_end[..., None]
    d_wend = jnp.sum(d_weighted * x_float, axis=3)
    d_cum_block, d_step_block = end_back((d_wend, d_decay))
    affinity_b = d_affinity.astype(bf16)
    d_read = (
        jnp.einsum("bts,bsn->btn", affinity_b, write_rows, preferred_element_type=f32)
        + d_read_state
    )
    d_write = (
        jnp.einsum("bts,btn->bsn", affinity_b, read_rows, preferred_element_type=f32)
        + dwrite_state
    )
    dx_total = dx_within + dx_state + d_skip[:, None] * dy_float
    d_act = jnp.concatenate(
        [dx_total.reshape(batch, block_len, inner_width), d_write, d_read], axis=2
    )
    d_ext, d_dtraw, d_convw, d_convb, d_dtbias, d_alog = mixer_back(
        (d_act, d_step_mix + d_step_block, d_cum_mix + d_cum_state + d_cum_block)
    )
    rim_grad = shifted(d_ext[:, :3], "seq", -1)
    d_xbc = d_ext[:, 3:] + jnp.pad(rim_grad, ((0, 0), (block_len - 3, 0), (0, 0)))
    d_proj = jnp.concatenate([grad_z, d_xbc, d_dtraw], axis=2).astype(bf16)
    d_normed = lax.dot_general(
        d_proj, w_in_all, (((2,), (1,)), ((), ())), preferred_element_type=f32
    )
    dx_norm, grad_gain = norm_back(d_normed)
    grad_rows = (cot_f + dx_norm).astype(bf16)
    grad_win = lax.dot_general(
        normed_b, d_proj, (((0, 1), (0, 1)), ((), ())), preferred_element_type=f32
    ).astype(bf16)

    heads = jnp.concatenate([d_dtbias, d_alog, grad_skip])
    pieces = jnp.concatenate(
        [
            grad_gain.reshape(all_devices, -1),
            d_convw.reshape(4, all_devices, -1).swapaxes(0, 1).reshape(all_devices, -1),
            d_convb.reshape(all_devices, -1),
            grad_gate.reshape(all_devices, -1),
            jnp.broadcast_to(heads, (all_devices, heads.size)),
        ],
        axis=1,
    )
    half = proj_width // 2
    grad_cols = -(-pieces.shape[1] // (2 * slab_rows))
    pieces = jnp.pad(pieces, ((0, 0), (0, 2 * grad_cols * slab_rows - pieces.shape[1])))
    halves = jnp.stack(
        [
            grad_win[:, :half].reshape(all_devices, slab_rows, half),
            grad_win[:, half:].reshape(all_devices, slab_rows, half),
        ],
        axis=1,
    )
    packed = jnp.concatenate(
        [halves, pieces.reshape(all_devices, 2, slab_rows, grad_cols).astype(bf16)], axis=3
    ).reshape(2 * model_width, half + grad_cols)
    summed = lax.psum_scatter(packed, axes, scatter_dimension=0, tiled=True).astype(f32)
    small_sum = summed[:, half:].reshape(-1)
    grad_win_own = jnp.concatenate([summed[:slab_rows, :half], summed[slab_rows:, :half]], axis=1)
    ends = bounds + [bounds[-1] + head_count * i for i in (1, 2, 3)]
    part = [small_sum[ends[i] : ends[i + 1]] for i in range(7)]
    return (
        result_rows,
        grad_rows,
        part[0],
        grad_win_own,
        part[1].reshape(4, -1),
        part[2],
        part[4],
        part[5],
        part[6],
        part[3],
        grad_wout,
    )


def solution(mesh):
    placed = (
        P("dp", "seq", None),
        P("dp", "seq", None),
        P("dp", None),
        P(("dp", "seq")),
        P(("dp", "seq"), None),
        P(None, ("dp", "seq")),
        P(("dp", "seq")),
        P(),
        P(),
        P(),
        P(("dp", "seq")),
        P(("dp", "seq"), None),
    )
    return jax.shard_map(
        per_device,
        mesh=mesh,
        in_specs=placed,
        out_specs=(
            P("dp", "seq", None),
            P("dp", "seq", None),
            P(("dp", "seq")),
            P(("dp", "seq"), None),
            P(None, ("dp", "seq")),
            P(("dp", "seq")),
            P(),
            P(),
            P(),
            P(("dp", "seq")),
            P(("dp", "seq"), None),
        ),
        check_vma=False,
    )
```

time: 913 us -> 577 us (0.63)
  blocking collectives: 273 us -> 0 us
  waiting for transfers between devices: 308 us -> 180 us
  local copies, waits for them, and re-layouts: 48.2 us -> 121 us
  other arithmetic: 128 us -> 155 us
  matrix products: 89.8 us -> 71.4 us
  starting transfers between devices: 44.1 us -> 27 us
    unnamed x3 -> x4, waiting for transfers between devices: 148 us -> 0.74 us
    all_gather x2 -> x0, blocking collectives: 134 us -> none  [accumulate(): lax.all_gather(conv_weight, ('dp', 'seq'), axis=1, tiled=True)]
    ppermute x16 -> x2, waiting for transfers between devices: 97.6 us -> 0.01 us  [shifted(): lax.ppermute(value, axis, [(source, source + steps) for source in range(i...]
    while x2 -> x0, blocking collectives: 90.3 us -> none
    all_gather x4 -> x2, waiting for transfers between devices: 0.01 us -> 56.7 us  [the longest x1 56.7 us: per_device(): lax.all_gather(jnp.concatenate([w_in, smalls], axis=1), axes, axis=0, til...]
    unnamed x1 -> x0, blocking collectives: 49.2 us -> none
    reduce_scatter x1 -> x2, waiting for transfers between devices: 59.6 us -> 102 us  [the longest x1 102 us: per_device(): lax.psum_scatter(packed, axes, scatter_dimension=0, tiled=True).astype(f32)]
    ppermute x16 -> x2, starting transfers between devices: 43.9 us -> 6.39 us  [shifted(): lax.ppermute(value, axis, [(source, source + steps) for source in range(i...]
  transfers between devices with their start and end apart: 22 -> 18, of which waited for: 16 -> 5; matrix products, arithmetic and copies ran while one was open for 13% -> 47% of each run, Pallas kernels for 0% -> 0%
where the time goes in v1:
time: 577 us; the launch traced here: 569 us
  waiting for transfers between devices  180 us (31%)
  other arithmetic  155 us (27%)
  local copies, waits for them, and re-layouts  121 us (21%)
  matrix products  71.4 us (12%)
  starting transfers between devices  27 us (5%)
  between operations  15.6 us (3%)
    reduce_scatter x1, waiting for transfers between devices, per_device(): lax.psum_scatter(packed, axes, scatter_dimension=0, tiled=True).astype(f32)  102 us
    all_gather x1, waiting for transfers between devices, per_device(): lax.all_gather(jnp.concatenate([w_in, smalls], axis=1), axes, axis=0, til...  56.7 us
    ppermute x12, starting transfers between devices, hop(): return lax.ppermute(value, axis, [(source, target)])  20.5 us
    ppermute x12, waiting for transfers between devices, hop(): return lax.ppermute(value, axis, [(source, target)])  20.5 us
    reduce_sum x1, other arithmetic, mixer_inputs(): conv_w[offset] * xbc_ext[:, offset:offset + block_len]  19.9 us
    reduce_sum x2, other arithmetic, per_device(): grad_skip = jnp.sum(dy_float * x_float, axis=(0, 1, 3))  17.4 us
    another operation x9, other arithmetic  13.8 us
    convert_element_type x1, other arithmetic, per_device(): act_b = activated.astype(bf16)  12.7 us
  transfers between devices with their start and end apart: 18, of which 5 were waited for; matrix products, arithmetic and copies ran while one was open for 47% of the time, Pallas kernels for 0%

profile of v1, /device:TPU:0, one launch (start us, length us, event | category | flops | bytes accessed | tf_op | source)
XLA Modules:
  0.0 569.2 jit_solution(12078500677821389656)
XLA Ops:
  23.6 56.7 %all-gather.3.cloned.1.call-done = bf16[768,3367]{1,0:T(8,128)(2,1)} async-done(((bf16[24,3367]{1,0:T(8,128)(2,1)}), bf16[768,3367]{1,0:T(8,128)(2,1)}) %all-gather.3.cloned.1.call-update) | async-done | bytes 5171728 | tf_op jit(solution)/shard_map/all_gather | solution.py:120
  83.6 7.5 %fusion.10 = bf16[2,256,3352]{1,2,0:T(8,128)(2,1)} fusion(bf16[768,3367]{1,0:T(8,128)(2,1)} %all-gather.3.cloned.1.call-done, bf16[2,256,768]{2,1,0:T(8,128)(2,1)} %param.12, f32[768]{0:T(1024)S(1)} %reshape.324, f32[2,256]{1,0:T(2,128)S(1)} %fusion.81), kind=kOutput, calls=%fused_computation.32 | convolution fusion | flops 2637692928 | bytes 9395712 | tf_op jit(solution)/shard_map/dot_general | solution.py:143
  91.2 8.8 %copy.283 = bf16[2,256,3352]{2,0,1:T(2,128)(2,1)S(1)} copy(bf16[2,256,3352]{1,2,0:T(8,128)(2,1)} %fusion.10) | data formatting | bytes 6864896 | tf_op jit(solution)/shard_map/dot_general | solution.py:143
  100.6 4.6 collective-permute-start
  135.6 12.7 %multiply_convert_fusion.6 = (bf16[2,256,1792]{2,0,1:T(2,128)(2,1)S(1)}, f32[2,256,1792]{2,0,1:T(2,128)}) fusion(f32[2,256]{0,1:T(8,128)S(1)} %copy-done.31, f32[2,259,1792]{2,0,1:T(2,128)S(1)} %maximum_convert_fusion, f32[1792]{0:T(1024)S(1)} %mul.600, f32[2,256]{0,1:T(8,128)S(1)} %copy-done.29, f32[1792]{0:T(1024)S(1)} %mul.594, ...), kind=kLoop, calls=%fused_computation.43 | loop fusion | flops 15597568 | bytes 20229120 | tf_op jit(solution)/shard_map/convert_element_type | solution.py:165
  159.3 8.4 %collective-permute-done.1 = bf16[24,64,128]{2,1,0:T(8,128)(2,1)S(1)} collective-permute-done((bf16[24,64,128]{2,1,0:T(8,128)(2,1)S(1)}, bf16[24,64,128]{2,1,0:T(8,128)(2,1)S(1)}, u32[]{:S(2)}, u32[]{:S(2)}) %collective-permute-start.1) | collective-permute-done | bytes 393248 | tf_op jit(solution)/shard_map/ppermute | solution.py:14
  170.2 5.8 %collective-permute-start.4 = (bf16[24,64,128]{2,1,0:T(8,128)(2,1)}, bf16[24,64,128]{2,1,0:T(8,128)(2,1)}, u32[]{:S(2)}, u32[]{:S(2)}) collective-permute-start(bf16[24,64,128]{2,1,0:T(8,128)(2,1)} %get-tuple-element.64), channel_id=1, source_target_pairs={{0,1},{4,5},{8,9},{12,13},{16,17},{20,21},{24,25},{28,29}} | collective-permute-start | bytes 1179656 | tf_op jit(solution)/shard_map/ppermute | solution.py:14
  176.8 5.0 fusion.28
  201.6 5.9 %fusion.6 = f32[2,24,64,256]{3,2,1,0:T(8,128)} fusion(bf16[2,256,24,64]{1,3,2,0:T(8,128)(2,1)S(1)} %bitcast.178, f32[2,24,256]{2,1,0:T(8,128)} %copy.295, f32[2,24,256]{2,1,0:T(8,128)} %copy.293, f32[2,256,256]{2,1,0:T(8,128)S(1)} %fusion.100, pred[2,256,256]{2,1,0:T(8,128)(4,1)} %compare_and_fusion), kind=kOutput, calls=%fused_computation.18 | convolution fusion | flops 418381824 | bytes 5472256 | tf_op jit(solution)/shard_map/bhts,bshp->bthp/dot_general | solution.py:190
  215.0 4.3 copy.303
  219.2 7.3 %multiply_reduce_fusion.9 = (f32[2,256]{0,1:T(8,128)}, f32[2,256,1536]{2,0,1:T(2,128)}) fusion(f32[2,256,1536]{2,0,1:T(2,128)S(1)} %copy.303, bf16[2,256,3352]{2,0,1:T(2,128)(2,1)} %copy-done.3), kind=kLoop, calls=%fused_computation.63 | loop fusion | flops 6290944 | bytes 7866368 | tf_op jit(solution)/shard_map/jvp()/reduce_sum | solution.py:67
  230.9 10.3 %multiply_reduce_fusion.7 = (bf16[1536]{0:T(1024)(128)(2,1)}, f32[2,256]{0,1:T(8,128)}) fusion(f32[2,256,1536]{2,1,0:T(8,128)} %fusion.28, f32[2,256,1536]{2,0,1:T(2,128)} %get-tuple-element.38, f32[2,256]{0,1:T(8,128)} %copy.305, f32[1536]{0:T(1024)S(1)} %reshape.325), kind=kLoop, calls=%fused_computation.59 | loop fusion | flops 4716544 | bytes 6304768 | tf_op jit(solution)/shard_map/transpose(jvp())/reduce_sum | solution.py:66
  245.4 16.7 %multiply_reduce_fusion.6 = (f32[1536]{0:T(1024)}, bf16[2,256,1536]{2,0,1:T(2,128)(2,1)}, bf16[2,256,1536]{2,0,1:T(2,128)(2,1)}, bf16[2,256,1536]{2,0,1:T(2,128)(2,1)}) fusion(bf16[2,256,1792]{2,0,1:T(2,128)(2,1)} %copy-done.4, bf16[2,256,3352]{2,0,1:T(2,128)(2,1)} %copy-done.3, f32[2,256,1536]{2,0,1:T(2,128)} %get-tuple-element.38, f32[2,256]{0,1:T(8,128)} %copy.309, ...), kind=kLoop, calls=%fused_computation.58 | loop fusion | flops 21232128 | bytes 17317888 | tf_op jit(solution)/shard_map/reduce_sum | solution.py:217
  262.2 4.9 copy.311
  271.2 10.3 %fusion.2 = (f32[2,24,256]{2,1,0:T(8,128)}, f32[2,24,256]{2,1,0:T(8,128)}, f32[2,24,256]{2,1,0:T(8,128)}, bf16[2,256,256]{2,1,0:T(8,128)(2,1)S(1)}) fusion(f32[2,24,256]{2,1,0:T(8,128)S(1)} %copy-done.69, f32[2,24,256]{2,1,0:T(8,128)S(1)} %copy-done.67, f32[2,256,256]{2,1,0:T(8,128)S(1)} %copy-done.53, pred[2,256,256]{2,1,0:T(8,128)(4,1)S(1)} %copy-done.59, ...), kind=kOutput, calls=%fused_computation.8 | convolution fusion | flops 443379712 | bytes 4308992 | tf_op jit(solution)/shard_map/bthp,bshp->bhts/dot_general | solution.py:218
  298.7 4.9 copy.338
  303.6 4.5 bitcast_convert_fusion.1
  319.1 8.1 %collective-permute-done.9 = bf16[24,64,128]{2,1,0:T(8,128)(2,1)} collective-permute-done((bf16[24,64,128]{2,1,0:T(8,128)(2,1)}, bf16[24,64,128]{2,1,0:T(8,128)(2,1)}, u32[]{:S(2)}, u32[]{:S(2)}) %collective-permute-start.9) | collective-permute-done | bytes 393248 | tf_op jit(solution)/shard_map/ppermute | solution.py:14
  337.7 5.1 fusion.23
  342.8 4.3 copy.320
  348.5 19.9 %multiply_reduce_fusion.5 = (f32[1792]{0:T(1024)}, f32[1792]{0:T(1024)}, f32[1792]{0:T(1024)}, f32[1792]{0:T(1024)}, bf16[1792]{0:T(1024)(128)(2,1)}, /*index=5*/f32[2,256,1792]{2,0,1:T(2,128)S(1)}) fusion(f32[2,259,1792]{2,0,1:T(2,128)} %copy-done, f32[2,256]{0,1:T(8,128)} %copy.287, f32[2,256]{0,1:T(8,128)} %copy.286, f32[2,256]{0,1:T(8,128)} %copy.285, ...), kind=kLoop, calls=%fused_computation.42 | loop fusion | flops 22011136 | bytes 25730560 | tf_op jit(solution)/shard_map/transpose(jvp())/reduce_sum | solution.py:34
  368.5 6.0 %multiply_multiply_fusion.3 = (f32[2,256,1792]{2,0,1:T(2,128)S(1)}, f32[2,256,1792]{2,0,1:T(2,128)S(1)}, f32[2,256,1792]{2,0,1:T(2,128)S(1)}, f32[2,256,1792]{2,0,1:T(2,128)S(1)}) fusion(f32[2,256,1792]{2,0,1:T(2,128)S(1)} %get-tuple-element.36, f32[2,256]{0,1:T(8,128)S(1)} %copy-done.32, f32[1792]{0:T(1024)S(1)} %copy-done.66, f32[2,256]{0,1:T(8,128)S(1)} %copy-done.26, ...), kind=kLoop, calls=%fused_computation.76 | loop fusion | flops 7340032 | bytes 18386944 | tf_op jit(solution)/shard_map/transpose(jvp())/mul | solution.py:34
  374.5 6.7 %pad_add_fusion = f32[2,259,1792]{2,0,1:T(2,128)} fusion(f32[2,256,1792]{2,0,1:T(2,128)S(1)} %get-tuple-element.49, f32[2,256,1792]{2,0,1:T(2,128)S(1)} %get-tuple-element.50, f32[2,256,1792]{2,0,1:T(2,128)S(1)} %get-tuple-element.51, f32[2,256,1792]{2,0,1:T(2,128)S(1)} %get-tuple-element.48), kind=kLoop, calls=%fused_computation.33 | loop fusion | flops 2784768 | bytes 18393088 | tf_op jit(solution)/shard_map/transpose(jvp())/add_any | solution.py:35
  384.8 5.0 reduce-window.16
  397.6 6.0 %pad_maximum_fusion.3 = bf16[2,256,3352]{2,0,1:T(2,128)(2,1)S(1)} fusion(bf16[2,256,24]{2,0,1:T(2,128)(2,1)S(1)} %copy-done.51, bf16[2,256,1792]{2,0,1:T(2,128)(2,1)S(1)} %fusion.13, bf16[2,256,1536]{2,0,1:T(2,128)(2,1)} %get-tuple-element.45), kind=kLoop, calls=%fused_computation.46 | loop fusion | flops 10297344 | bytes 6864896 | tf_op jit(solution)/shard_map/concatenate | solution.py:248
  403.6 7.3 %copy.331 = bf16[2,256,3352]{1,2,0:T(8,128)(2,1)} copy(bf16[2,256,3352]{2,0,1:T(2,128)(2,1)S(1)} %pad_maximum_fusion.3) | data formatting | bytes 6864896 | tf_op jit(solution)/shard_map/concatenate | solution.py:248
  410.9 5.2 bitcast_convert_fusion
  422.5 4.8 copy.334
  433.7 7.1 %fusion.36 = (bf16[768]{0:T(1024)(128)(2,1)S(1)}, f32[2,256]{1,0:T(2,128)S(1)}, f32[2,256,768]{2,1,0:T(8,128)}) fusion(bf16[2,256,768]{2,1,0:T(8,128)(2,1)S(1)} %copy-done.17, f32[2,256]{1,0:T(2,128)S(1)} %copy-done.98, f32[768]{0:T(1024)S(1)} %copy-done.88, bf16[2,256,3352]{1,2,0:T(8,128)(2,1)S(1)} %copy-done.24, ...), kind=kOutput, calls=%fused_computation.88 | convolution fusion | flops 2638871296 | bytes 10972160 | tf_op jit(solution)/shard_map/dot_general | solution.py:249
  441.4 5.5 pad_maximum_fusion.1
  448.3 4.1 fusion.40
  455.5 101.8 %reduce-scatter.3.cloned.1.call-done = bf16[48,1685]{1,0:T(8,128)(2,1)} async-done(((bf16[1536,1685]{1,0:T(8,128)(2,1)}), bf16[48,1685]{1,0:T(8,128)(2,1)}) %reduce-scatter.3.cloned.1.call-update) | async-done | bytes 161776 | tf_op jit(solution)/shard_map/reduce_scatter | solution.py:282
  (411 shorter events, 178.4 us)
Async XLA Ops:
  7.2 73.2 %all-gather.3.cloned.1.call-start = ((), (), s32[]{:S(2)}) async-start(), calls=%async_computation.2 | async-start | bytes 5474304 | tf_op jit(solution)/shard_map/all_gather | solution.py:120
  11.9 164.9 %all-gather.5.cloned.1.call-start = ((), (), s32[]{:S(2)}) async-start(), calls=%async_computation.3 | async-start | bytes 2433024 | tf_op jit(solution)/shard_map/all_gather | solution.py:123
  12.6 441.3 %reduce-scatter.5.cloned.1.call-start = ((), (), s32[]{:S(2)}) async-start(), calls=%async_computation.5 | async-start | bytes 2433024 | tf_op jit(solution)/shard_map/reduce_scatter | solution.py:208
  16.8 101.0 %copy-start.108 = (f32[2]{0:T(128)}, f32[2]{0:T(128)S(1)}, u32[]{:S(2)}) copy-start(f32[2]{0:T(128)S(1)} %slice_reduce_fusion.6) | copy-start | bytes 28
  22.1 60.9 %copy-start.97 = (f32[2,256]{1,0:T(2,128)}, f32[2,256]{1,0:T(2,128)S(1)}, u32[]{:S(2)}) copy-start(f32[2,256]{1,0:T(2,128)S(1)} %fusion.81) | copy-start | bytes 6148
  22.8 83.9 %copy-start.106 = (f32[24]{0:T(128)}, f32[24]{0:T(128)S(1)}, u32[]{:S(2)}) copy-start(f32[24]{0:T(128)S(1)} %exponential_negate_fusion) | copy-start | bytes 292
  99.9 26.4 %copy-start.3 = (bf16[2,256,3352]{2,0,1:T(2,128)(2,1)}, bf16[2,256,3352]{2,0,1:T(2,128)(2,1)S(1)}, u32[]{:S(2)}) copy-start(bf16[2,256,3352]{2,0,1:T(2,128)(2,1)S(1)} %copy.283) | copy-start | bytes 10297348
  100.6 31.5 %collective-permute-start = (bf16[2,3,1792]{2,0,1:T(2,128)(2,1)}, bf16[2,3,1792]{2,0,1:T(2,128)(2,1)}, u32[]{:S(2)}, u32[]{:S(2)}) collective-permute-start(bf16[2,3,1792]{2,0,1:T(2,128)(2,1)} %slice.260), channel_id=1, source_target_pairs={{0,1},{1,2},{2,3},{4,5},{5,6},{6,7},{8,9},{9,10},{10,11},{12,13},{... | collective-permute-start | bytes 64520 | tf_op jit(solution)/shard_map/ppermute | solution.py:20
  128.0 20.3 %copy-start.61 = (f32[1792]{0:T(1024)}, f32[1792]{0:T(1024)S(1)}, u32[]{:S(2)}) copy-start(f32[1792]{0:T(1024)S(1)} %mul.588) | copy-start | bytes 21508
  154.2 57.4 %copy-start.1 = (bf16[2,256,1536]{1,2,0:T(8,128)(2,1)}, bf16[2,256,1536]{1,2,0:T(8,128)(2,1)S(1)}, u32[]{:S(2)}) copy-start(bf16[2,256,1536]{1,2,0:T(8,128)(2,1)S(1)} %copy.288) | copy-start | bytes 4718596
  155.4 20.5 %copy-start.79 = (s32[2,256]{1,0:T(2,128)S(1)}, s32[2,256]{1,0:T(2,128)}, u32[]{:S(2)}) copy-start(s32[2,256]{1,0:T(2,128)} %copy-done.78) | copy-start | bytes 6148
  157.1 10.7 %collective-permute-start.1 = (bf16[24,64,128]{2,1,0:T(8,128)(2,1)S(1)}, bf16[24,64,128]{2,1,0:T(8,128)(2,1)S(1)}, u32[]{:S(2)}, u32[]{:S(2)}) collective-permute-start(bf16[24,64,128]{2,1,0:T(8,128)(2,1)S(1)} %add_convert_fusion.7), channel_id=1, source_target_pairs={{0,1},{4,5},{8,9},{12,13},{16,17},{20,21},{24,25},{28,29}} | collective-permute-start | bytes 1179656 | tf_op jit(solution)/shard_map/ppermute | solution.py:14
  159.3 26.6 %copy-start.90 = (f32[24]{0:T(128)}, f32[24]{0:T(128)S(1)}, u32[]{:S(2)}) copy-start(f32[24]{0:T(128)S(1)} %get-tuple-element.83) | copy-start | bytes 292
  168.8 17.1 %collective-permute-start.2 = (bf16[24,64,128]{2,1,0:T(8,128)(2,1)}, bf16[24,64,128]{2,1,0:T(8,128)(2,1)}, u32[]{:S(2)}, u32[]{:S(2)}) collective-permute-start(bf16[24,64,128]{2,1,0:T(8,128)(2,1)} %get-tuple-element.63), channel_id=1, source_target_pairs={{1,2},{5,6},{9,10},{13,14},{17,18},{21,22},{25,26},{29,30}} | collective-permute-start | bytes 1179656 | tf_op jit(solution)/shard_map/ppermute | solution.py:14
  170.2 15.7 %collective-permute-start.4 = (bf16[24,64,128]{2,1,0:T(8,128)(2,1)}, bf16[24,64,128]{2,1,0:T(8,128)(2,1)}, u32[]{:S(2)}, u32[]{:S(2)}) collective-permute-start(bf16[24,64,128]{2,1,0:T(8,128)(2,1)} %get-tuple-element.64), channel_id=1, source_target_pairs={{0,1},{4,5},{8,9},{12,13},{16,17},{20,21},{24,25},{28,29}} | collective-permute-start | bytes 1179656 | tf_op jit(solution)/shard_map/ppermute | solution.py:14
  188.3 9.7 %collective-permute-start.5 = (bf16[24,64,128]{2,1,0:T(8,128)(2,1)}, bf16[24,64,128]{2,1,0:T(8,128)(2,1)}, u32[]{:S(2)}, u32[]{:S(2)}) collective-permute-start(bf16[24,64,128]{2,1,0:T(8,128)(2,1)} %get-tuple-element.62), channel_id=1, source_target_pairs={{1,2},{5,6},{9,10},{13,14},{17,18},{21,22},{25,26},{29,30}} | collective-permute-start | bytes 1179656 | tf_op jit(solution)/shard_map/ppermute | solution.py:14
  196.5 11.9 %collective-permute-start.3 = (bf16[24,64,128]{2,1,0:T(8,128)(2,1)}, bf16[24,64,128]{2,1,0:T(8,128)(2,1)}, u32[]{:S(2)}, u32[]{:S(2)}) collective-permute-start(bf16[24,64,128]{2,1,0:T(8,128)(2,1)} %get-tuple-element.61), channel_id=1, source_target_pairs={{2,3},{6,7},{10,11},{14,15},{18,19},{22,23},{26,27},{30,31}} | collective-permute-start | bytes 1179656 | tf_op jit(solution)/shard_map/ppermute | solution.py:14
  200.1 9.7 %collective-permute-start.6 = (bf16[24,64,128]{2,1,0:T(8,128)(2,1)}, bf16[24,64,128]{2,1,0:T(8,128)(2,1)}, u32[]{:S(2)}, u32[]{:S(2)}) collective-permute-start(bf16[24,64,128]{2,1,0:T(8,128)(2,1)} %add_convert_fusion.4), channel_id=1, source_target_pairs={{2,3},{6,7},{10,11},{14,15},{18,19},{22,23},{26,27},{30,31}} | collective-permute-start | bytes 1179656 | tf_op jit(solution)/shard_map/ppermute | solution.py:14
  270.1 11.4 %collective-permute-start.7 = (bf16[24,64,128]{2,1,0:T(8,128)(2,1)S(1)}, bf16[24,64,128]{2,1,0:T(8,128)(2,1)S(1)}, u32[]{:S(2)}, u32[]{:S(2)}) collective-permute-start(bf16[24,64,128]{2,1,0:T(8,128)(2,1)S(1)} %add_convert_fusion.3), channel_id=1, source_target_pairs={{3,2},{7,6},{11,10},{15,14},{19,18},{23,22},{27,26},{31,30}} | collective-permute-start | bytes 1179656 | tf_op jit(solution)/shard_map/ppermute | solution.py:14
  281.8 4.6 collective-permute-start.10
  282.6 3.8 collective-permute-start.8
  287.7 21.6 %collective-permute-start.11 = (bf16[24,64,128]{2,1,0:T(8,128)(2,1)}, bf16[24,64,128]{2,1,0:T(8,128)(2,1)}, u32[]{:S(2)}, u32[]{:S(2)}) collective-permute-start(bf16[24,64,128]{2,1,0:T(8,128)(2,1)} %get-tuple-element.58), channel_id=1, source_target_pairs={{2,1},{6,5},{10,9},{14,13},{18,17},{22,21},{26,25},{30,29}} | collective-permute-start | bytes 1179656 | tf_op jit(solution)/shard_map/ppermute | solution.py:14
  308.0 19.2 %collective-permute-start.9 = (bf16[24,64,128]{2,1,0:T(8,128)(2,1)}, bf16[24,64,128]{2,1,0:T(8,128)(2,1)}, u32[]{:S(2)}, u32[]{:S(2)}) collective-permute-start(bf16[24,64,128]{2,1,0:T(8,128)(2,1)} %get-tuple-element.57), channel_id=1, source_target_pairs={{1,0},{5,4},{9,8},{13,12},{17,16},{21,20},{25,24},{29,28}} | collective-permute-start | bytes 1179656 | tf_op jit(solution)/shard_map/ppermute | solution.py:14
  311.4 21.0 %collective-permute-start.12 = (bf16[24,64,128]{2,1,0:T(8,128)(2,1)}, bf16[24,64,128]{2,1,0:T(8,128)(2,1)}, u32[]{:S(2)}, u32[]{:S(2)}) collective-permute-start(bf16[24,64,128]{2,1,0:T(8,128)(2,1)} %add_convert_fusion), channel_id=1, source_target_pairs={{1,0},{5,4},{9,8},{13,12},{17,16},{21,20},{25,24},{29,28}} | collective-permute-start | bytes 1179656 | tf_op jit(solution)/shard_map/ppermute | solution.py:14
  318.2 239.0 %reduce-scatter.3.cloned.1.call-start = ((), (), s32[]{:S(2)}) async-start(), calls=%async_computation.4 | async-start | bytes 5677056 | tf_op jit(solution)/shard_map/reduce_scatter | solution.py:282
  348.4 20.0 %copy-start.28 = (f32[2,256]{0,1:T(8,128)S(1)}, f32[2,256]{0,1:T(8,128)}, u32[]{:S(2)}) copy-start(f32[2,256]{0,1:T(8,128)} %copy.285) | copy-start | bytes 6148
  348.4 20.0 %copy-start.30 = (f32[2,256]{0,1:T(8,128)S(1)}, f32[2,256]{0,1:T(8,128)}, u32[]{:S(2)}) copy-start(f32[2,256]{0,1:T(8,128)} %copy.286) | copy-start | bytes 6148
  348.5 20.0 %copy-start.32 = (f32[2,256]{0,1:T(8,128)S(1)}, f32[2,256]{0,1:T(8,128)}, u32[]{:S(2)}) copy-start(f32[2,256]{0,1:T(8,128)} %copy.287) | copy-start | bytes 6148
  348.5 20.0 %copy-start.62 = (f32[1792]{0:T(1024)S(1)}, f32[1792]{0:T(1024)}, u32[]{:S(2)}) copy-start(f32[1792]{0:T(1024)} %copy-done.61) | copy-start | bytes 21508
  348.5 20.0 %copy-start.64 = (f32[1792]{0:T(1024)S(1)}, f32[1792]{0:T(1024)}, u32[]{:S(2)}) copy-start(f32[1792]{0:T(1024)} %copy-done.63) | copy-start | bytes 21508
  348.5 20.0 %copy-start.66 = (f32[1792]{0:T(1024)S(1)}, f32[1792]{0:T(1024)}, u32[]{:S(2)}) copy-start(f32[1792]{0:T(1024)} %copy-done.65) | copy-start | bytes 21508
  381.7 12.6 %collective-permute-start.13 = (f32[2,3,1792]{2,0,1:T(2,128)S(1)}, f32[2,3,1792]{2,0,1:T(2,128)S(1)}, u32[]{:S(2)}, u32[]{:S(2)}) collective-permute-start(f32[2,3,1792]{2,0,1:T(2,128)S(1)} %pad_add_fusion.1), channel_id=1, source_target_pairs={{1,0},{2,1},{3,2},{5,4},{6,5},{7,6},{9,8},{10,9},{11,10},{13,12},{... | collective-permute-start | bytes 129032 | tf_op jit(solution)/shard_map/ppermute | solution.py:20
  (99 other events, 617.0 us)
Sparse Core Ops, SparseCore 0:
  12.0 68.3 all-gather.2
  83.1 55.4 all-gather.4
  318.3 107.1 reduce-scatter.4
  447.1 110.1 reduce-scatter.2

commit v2 on v1

--- a/solution.py
+++ b/solution.py
@@ -117,12 +117,17 @@
         [norm_gain, conv_weight.reshape(-1), conv_bias, gate_gain,
          jnp.zeros((small_cols * slab_rows - sum(small_sizes),), bf16)]
     ).reshape(slab_rows, small_cols)
-    w_in_full = lax.all_gather(
-        jnp.concatenate([w_in, smalls], axis=1), axes, axis=0, tiled=True
-    )
-    w_out_all = lax.all_gather(w_out, axes, axis=0, tiled=True)
-    w_in_all = w_in_full[:, :proj_width]
-    small_all = w_in_full[:, proj_width:].reshape(all_devices, slab_rows * small_cols)
+    rest_width = proj_width - inner_width
+    w_rest_full = lax.all_gather(
+        jnp.concatenate([w_in[:, inner_width:], smalls], axis=1), axes, axis=0, tiled=True
+    )
+    w_rest_full, w_gate_own, w_out_own = lax.optimization_barrier(
+        (w_rest_full, w_in[:, :inner_width], w_out)
+    )
+    w_gate_all = lax.all_gather(w_gate_own, axes, axis=0, tiled=True)
+    w_out_all = lax.all_gather(w_out_own, axes, axis=0, tiled=True)
+    w_rest_all = w_rest_full[:, :rest_width]
+    small_all = w_rest_full[:, rest_width:].reshape(all_devices, slab_rows * small_cols)
     bounds = [0]
     for size in small_sizes:
         bounds.append(bounds[-1] + size)
@@ -141,9 +146,12 @@
     normed, norm_back = jax.vjp(norm_input, tokens_f, gain_all)
     normed_b = normed.astype(bf16)
     projected = lax.dot_general(
-        normed_b, w_in_all, (((2,), (0,)), ((), ())), preferred_element_type=f32
-    ).astype(bf16)
-    xbc_rows = projected[:, :, inner_width : inner_width + xbc_width]
+        normed_b, w_rest_all, (((2,), (0,)), ((), ())), preferred_element_type=f32
+    ).astype(bf16)
+    z_rows = lax.dot_general(
+        normed_b, w_gate_all, (((2,), (0,)), ((), ())), preferred_element_type=f32
+    ).astype(bf16)
+    xbc_rows = projected[:, :, :xbc_width]
     rim_rows = shifted(xbc_rows[:, block_len - 3 :], "seq", 1)
     padded = jnp.concatenate([jnp.full((batch, 3), -1, jnp.int32), segments], axis=1)
     seg_window = lax.dynamic_slice_in_dim(padded, block_start, block_len + 3, axis=1)
@@ -152,7 +160,7 @@
         [seg_window[:, offset : offset + block_len] == seg_local for offset in range(4)], axis=2
     ).astype(f32)
     xbc_ext = jnp.concatenate([rim_rows, xbc_rows], axis=1).astype(f32)
-    dt_raw = projected[:, :, inner_width + xbc_width :].astype(f32)
+    dt_raw = projected[:, :, xbc_width:].astype(f32)
     (activated, step_size, cumulated), mixer_back = jax.vjp(
         partial(mixer_inputs, tap_mask=tap_mask),
         xbc_ext,
@@ -192,7 +200,7 @@
     scaled_b = scaled.astype(bf16)
     from_state = jnp.einsum("bthn,bhpn->bthp", scaled_b, state_b, preferred_element_type=f32)
     y_heads = within + from_state + d_skip[:, None] * x_float
-    z_float = projected[:, :, :inner_width].astype(f32)
+    z_float = z_rows.astype(f32)
     gated, gate_back = jax.vjp(
         gate_norm, y_heads.reshape(batch, block_len, inner_width), z_float, gate_all
     )
@@ -205,16 +213,42 @@
     grad_wout = lax.dot_general(
         gated_b, cotangent, (((0, 1), (0, 1)), ((), ())), preferred_element_type=f32
     ).astype(bf16)
-    grad_wout = lax.psum_scatter(grad_wout, axes, scatter_dimension=0, tiled=True).astype(f32)
     d_gated = lax.dot_general(
         cotangent, w_out_all, (((2,), (1,)), ((), ())), preferred_element_type=f32
     )
     grad_y, grad_z, grad_gate = gate_back(d_gated)
-    dy_b = grad_y.astype(bf16).reshape(batch, block_len, head_count, head_width)
+    dz_b = grad_z.astype(bf16)
+
+    def halved(value):
+        half = value.shape[1] // 2
+        return jnp.stack(
+            [
+                value[:, :half].reshape(all_devices, slab_rows, half),
+                value[:, half:].reshape(all_devices, slab_rows, half),
+            ],
+            axis=1,
+        )
+
+    def unhalved(value):
+        return jnp.concatenate([value[:slab_rows], value[slab_rows:]], axis=1)
+
+    grad_wz = lax.dot_general(
+        normed_b, dz_b, (((0, 1), (0, 1)), ((), ())), preferred_element_type=f32
+    ).astype(bf16)
+    grad_wz = halved(grad_wz).reshape(2 * model_width, inner_width // 2)
+    dy_b, grad_wz, grad_wout = lax.optimization_barrier(
+        (grad_y.astype(bf16), grad_wz, grad_wout)
+    )
+    grad_wout = lax.psum_scatter(grad_wout, axes, scatter_dimension=0, tiled=True).astype(f32)
+    grad_wz = lax.psum_scatter(grad_wz, axes, scatter_dimension=0, tiled=True).astype(f32)
+    skip_cols = jnp.sum(
+        dy_b.astype(f32) * act_b[:, :, :inner_width].astype(f32), axis=(0, 1)
+    )
+    grad_skip = jnp.sum(skip_cols.reshape(head_count, head_width), axis=1)
+    dy_b = dy_b.reshape(batch, block_len, head_count, head_width)
     dy_float = dy_b.astype(f32)
     state_grad = jnp.einsum("bthn,bthp->bhpn", scaled_b, dy_b, preferred_element_type=f32)
     adjoint = relay(block_decay, state_grad, -1)
-    grad_skip = jnp.sum(dy_float * x_float, axis=(0, 1, 3))
     d_mixing = jnp.einsum("bthp,bshp->bhts", dy_b, x_values, preferred_element_type=f32)
     dx_within = jnp.einsum("bhts,bthp->bshp", mixing_b, dy_b, preferred_element_type=f32)
     d_affinity, d_cum_mix, d_step_mix = mixing_back(d_mixing)
@@ -245,14 +279,16 @@
     )
     rim_grad = shifted(d_ext[:, :3], "seq", -1)
     d_xbc = d_ext[:, 3:] + jnp.pad(rim_grad, ((0, 0), (block_len - 3, 0), (0, 0)))
-    d_proj = jnp.concatenate([grad_z, d_xbc, d_dtraw], axis=2).astype(bf16)
+    d_rest = jnp.concatenate([d_xbc, d_dtraw], axis=2).astype(bf16)
     d_normed = lax.dot_general(
-        d_proj, w_in_all, (((2,), (1,)), ((), ())), preferred_element_type=f32
+        dz_b, w_gate_all, (((2,), (1,)), ((), ())), preferred_element_type=f32
+    ) + lax.dot_general(
+        d_rest, w_rest_all, (((2,), (1,)), ((), ())), preferred_element_type=f32
     )
     dx_norm, grad_gain = norm_back(d_normed)
     grad_rows = (cot_f + dx_norm).astype(bf16)
-    grad_win = lax.dot_general(
-        normed_b, d_proj, (((0, 1), (0, 1)), ((), ())), preferred_element_type=f32
+    grad_rest = lax.dot_general(
+        normed_b, d_rest, (((0, 1), (0, 1)), ((), ())), preferred_element_type=f32
     ).astype(bf16)
 
     heads = jnp.concatenate([d_dtbias, d_alog, grad_skip])
@@ -266,22 +302,15 @@
         ],
         axis=1,
     )
-    half = proj_width // 2
+    half = rest_width // 2
     grad_cols = -(-pieces.shape[1] // (2 * slab_rows))
     pieces = jnp.pad(pieces, ((0, 0), (0, 2 * grad_cols * slab_rows - pieces.shape[1])))
-    halves = jnp.stack(
-        [
-            grad_win[:, :half].reshape(all_devices, slab_rows, half),
-            grad_win[:, half:].reshape(all_devices, slab_rows, half),
-        ],
-        axis=1,
-    )
     packed = jnp.concatenate(
-        [halves, pieces.reshape(all_devices, 2, slab_rows, grad_cols).astype(bf16)], axis=3
+        [halved(grad_rest), pieces.reshape(all_devices, 2, slab_rows, grad_cols).astype(bf16)], axis=3
     ).reshape(2 * model_width, half + grad_cols)
     summed = lax.psum_scatter(packed, axes, scatter_dimension=0, tiled=True).astype(f32)
     small_sum = summed[:, half:].reshape(-1)
-    grad_win_own = jnp.concatenate([summed[:slab_rows, :half], summed[slab_rows:, :half]], axis=1)
+    grad_win_own = jnp.concatenate([unhalved(grad_wz), unhalved(summed[:, :half])], axis=1)
     ends = bounds + [bounds[-1] + head_count * i for i in (1, 2, 3)]
     part = [small_sum[ends[i] : ends[i + 1]] for i in range(7)]
     return (

time: 577 us -> 595 us (1.031)
  waiting for transfers between devices: 180 us -> 234 us
  other arithmetic: 155 us -> 134 us
  local copies, waits for them, and re-layouts: 121 us -> 101 us
    reduce_scatter x0 -> x1, waiting for transfers between devices: none -> 24.4 us  [per_device(): lax.psum_scatter(grad_wz, axes, scatter_dimension=0, tiled=True).astype(f32)]
    ppermute x12, waiting for transfers between devices: 20.5 us -> 41.7 us  [hop(): return lax.ppermute(value, axis, [(source, target)])]
    reduce_sum x2, other arithmetic: 17.4 us -> 2.81 us  [the longest x1 2.18 us: per_device(): jnp.sum(dy_b.astype(f32) * act_b[:, :, :inner_width].astype(f32), axis=(0...]
    convert_element_type x0 -> x1, other arithmetic: none -> 13.6 us  [per_device(): grad_y.astype(bf16)]
    concatenate x4 -> x3, other arithmetic: 14 us -> 4.7 us  [the longest x1 2.14 us: per_device(): jnp.concatenate([halved(grad_rest), pieces.reshape(all_devices, 2, slab_r...]
    optimization_barrier x0 -> x2, local copies, waits for them, and re-layouts: none -> 7.71 us  [the longest x1 4.56 us: per_device(): lax.optimization_barrier((w_rest_full, w_in[:, :inner_width], w_out))]
    dot_general x3 -> x6, matrix products: 19.8 us -> 24.3 us  [the longest x1 6.6 us: per_device(): lax.dot_general(d_rest, w_rest_all, (((2,), (1,)), ((), ())), preferred_e...]
    another operation x10 -> x11, other arithmetic: 16.1 us -> 11.7 us
  transfers between devices with their start and end apart: 18 -> 20, of which waited for: 5 -> 8; matrix products, arithmetic and copies ran while one was open for 47% -> 42% of each run, Pallas kernels for 0% -> 0%
where the time goes in v2:
time: 595 us; the launch traced here: 586 us
  waiting for transfers between devices  234 us (39%)
  other arithmetic  134 us (23%)
  local copies, waits for them, and re-layouts  101 us (17%)
  matrix products  75.8 us (13%)
  starting transfers between devices  25.4 us (4%)
  between operations  16.3 us (3%)
    reduce_scatter x1, waiting for transfers between devices, per_device(): lax.psum_scatter(packed, axes, scatter_dimension=0, tiled=True).astype(f32)  106 us
    all_gather x1, waiting for transfers between devices, per_device(): lax.all_gather(jnp.concatenate([w_in[:, inner_width:], smalls], axis=1),...  60 us
    ppermute x12, waiting for transfers between devices, hop(): return lax.ppermute(value, axis, [(source, target)])  41.7 us
    reduce_scatter x1, waiting for transfers between devices, per_device(): lax.psum_scatter(grad_wz, axes, scatter_dimension=0, tiled=True).astype(f32)  24.4 us
    ppermute x12, starting transfers between devices, hop(): return lax.ppermute(value, axis, [(source, target)])  20.6 us
    reduce_sum x1, other arithmetic, mixer_inputs(): conv_w[offset] * xbc_ext[:, offset:offset + block_len]  19.7 us
    convert_element_type x1, other arithmetic, per_device(): grad_y.astype(bf16)  13.6 us
    convert_element_type x1, other arithmetic, per_device(): act_b = activated.astype(bf16)  12.7 us
  transfers between devices with their start and end apart: 20, of which 8 were waited for; matrix products, arithmetic and copies ran while one was open for 42% of the time, Pallas kernels for 0%

profile of v2, /device:TPU:0, one launch (start us, length us, event | category | flops | bytes accessed | tf_op | source)
XLA Modules:
  0.0 586.4 jit_solution(16949883693504555423)
XLA Ops:
  13.4 60.0 %all-gather.4.cloned.1.call-done = bf16[768,1831]{1,0:T(8,128)(2,1)} async-done(((bf16[24,1831]{1,0:T(8,128)(2,1)}), bf16[768,1831]{1,0:T(8,128)(2,1)}) %all-gather.4.cloned.1.call-update) | async-done | bytes 2812432 | tf_op jit(solution)/shard_map/all_gather | solution.py:121
  79.4 4.6 copy.309
  85.3 4.8 fusion.36
  90.1 5.1 copy.310
  110.6 3.4 maximum_convert_fusion
  114.0 12.7 %multiply_convert_fusion.6 = (bf16[2,256,1792]{2,0,1:T(2,128)(2,1)S(1)}, f32[2,256,1792]{2,0,1:T(2,128)}) fusion(f32[2,256]{0,1:T(8,128)S(1)} %copy.314, f32[2,259,1792]{2,0,1:T(2,128)S(1)} %maximum_convert_fusion, f32[1792]{0:T(1024)S(1)} %mul.599, f32[2,256]{0,1:T(8,128)S(1)} %copy.313, f32[1792]{0:T(1024)S(1)} %mul.593, f32[2,256]{0,1:T(8,128)S(1)} %copy.312, ...), kind=kLoop, calls=%fused_computation.39 | loop fusion | flops 15597568 | bytes 20229120 | tf_op jit(solution)/shard_map/convert_element_type | solution.py:173
  134.7 8.6 %collective-permute-done.1 = bf16[24,64,128]{2,1,0:T(8,128)(2,1)S(1)} collective-permute-done((bf16[24,64,128]{2,1,0:T(8,128)(2,1)S(1)}, bf16[24,64,128]{2,1,0:T(8,128)(2,1)S(1)}, u32[]{:S(2)}, u32[]{:S(2)}) %collective-permute-start.1) | collective-permute-done | bytes 393248 | tf_op jit(solution)/shard_map/ppermute | solution.py:14
  146.6 5.7 collective-permute-start.4
  176.7 5.9 %fusion.6 = f32[2,24,64,256]{3,2,1,0:T(8,128)} fusion(bf16[2,256,24,64]{1,3,2,0:T(8,128)(2,1)S(1)} %bitcast.201, f32[2,24,256]{2,1,0:T(8,128)} %copy.322, f32[2,24,256]{2,1,0:T(8,128)} %copy.320, f32[2,256,256]{2,1,0:T(8,128)S(1)} %fusion.112, pred[2,256,256]{2,1,0:T(8,128)(4,1)} %compare_and_fusion), kind=kOutput, calls=%fused_computation.16 | convolution fusion | flops 418381824 | bytes 5472256 | tf_op jit(solution)/shard_map/bhts,bshp->bthp/dot_general | solution.py:198
  190.0 4.3 copy.331
  194.3 5.0 fusion.27
  199.3 6.0 %copy.335 = f32[1536,2,256]{0,1,2:T(2,128)} copy(f32[1536,2,256]{2,0,1:T(8,128)} %fusion.27) | data formatting | bytes 6291456 | tf_op jit(solution)/shard_map/dot_general | solution.py:216
  208.7 7.1 %multiply_reduce_fusion.8 = (f32[2,256]{0,1:T(8,128)}, f32[2,256,1536]{2,0,1:T(2,128)}) fusion(f32[2,256,1536]{2,0,1:T(2,128)S(1)} %copy.331, bf16[2,256,1536]{2,1,0:T(8,128)(2,1)S(1)} %fusion.33), kind=kLoop, calls=%fused_computation.63 | loop fusion | flops 6290944 | bytes 7866368 | tf_op jit(solution)/shard_map/jvp()/reduce_sum | solution.py:67
  220.1 6.3 %fusion.22 = (bf16[1536]{0:T(1024)(128)(2,1)}, f32[2,256]{0,1:T(8,128)}) fusion(f32[1536,2,256]{0,1,2:T(2,128)} %copy.335, f32[2,256,1536]{2,0,1:T(2,128)} %get-tuple-element.48, f32[2,256]{0,1:T(8,128)} %copy.333, f32[1536]{0:T(1024)S(1)} %reshape.332), kind=kLoop, calls=%fused_computation.57 | loop fusion | flops 4716544 | bytes 6304768 | tf_op jit(solution)/shard_map/transpose(jvp())/reduce_sum | solution.py:66
  230.8 13.6 %multiply_convert_fusion.7 = (bf16[2,256,1536]{2,0,1:T(2,128)(2,1)}, bf16[2,256,1536]{2,0,1:T(2,128)(2,1)}, bf16[2,256,1536]{2,0,1:T(2,128)(2,1)}) fusion(f32[2,256,1536]{2,0,1:T(2,128)} %get-tuple-element.48, f32[2,256]{0,1:T(8,128)} %copy.337, f32[1536,2,256]{0,1,2:T(2,128)} %copy.335, f32[1536]{0:T(1024)S(1)} %reshape.332, f32[2,256]{0,1:T(8,128)} %copy.333, ...), kind=kLoop, calls=%fused_computation.60 | loop fusion | flops 18087936 | bytes 15738880 | tf_op jit(solution)/shard_map/convert_element_type | solution.py:240
  244.4 3.8 copy.343
  248.2 3.5 bitcast_convert_fusion.2
  267.5 10.4 %fusion.2 = (f32[2,24,256]{2,1,0:T(8,128)}, f32[2,24,256]{2,1,0:T(8,128)}, f32[2,24,256]{2,1,0:T(8,128)}, bf16[2,256,256]{2,1,0:T(8,128)(2,1)}) fusion(f32[2,24,256]{2,1,0:T(8,128)S(1)} %copy-done.70, f32[2,24,256]{2,1,0:T(8,128)S(1)} %copy-done.72, f32[2,256,256]{2,1,0:T(8,128)S(1)} %copy-done.55, pred[2,256,256]{2,1,0:T(8,128)(4,1)S(1)} %copy-done.61, ...), kind=kOutput, calls=%fused_computation.7 | convolution fusion | flops 443379712 | bytes 4308992 | tf_op jit(solution)/shard_map/bthp,bshp->bhts/dot_general | solution.py:252
  291.3 4.4 fusion.31
  312.3 17.2 %collective-permute-done.9 = bf16[24,64,128]{2,1,0:T(8,128)(2,1)} collective-permute-done((bf16[24,64,128]{2,1,0:T(8,128)(2,1)}, bf16[24,64,128]{2,1,0:T(8,128)(2,1)}, u32[]{:S(2)}, u32[]{:S(2)}) %collective-permute-start.9) | collective-permute-done | bytes 393248 | tf_op jit(solution)/shard_map/ppermute | solution.py:14
  330.9 12.4 %collective-permute-done.12 = bf16[24,64,128]{2,1,0:T(8,128)(2,1)} collective-permute-done((bf16[24,64,128]{2,1,0:T(8,128)(2,1)}, bf16[24,64,128]{2,1,0:T(8,128)(2,1)}, u32[]{:S(2)}, u32[]{:S(2)}) %collective-permute-start.12) | collective-permute-done | bytes 393248 | tf_op jit(solution)/shard_map/ppermute | solution.py:14
  349.3 5.1 fusion.21
  354.4 4.3 copy.353
  360.0 19.7 %multiply_reduce_fusion.5 = (f32[1792]{0:T(1024)}, f32[1792]{0:T(1024)}, f32[1792]{0:T(1024)}, f32[1792]{0:T(1024)}, bf16[1792]{0:T(1024)(128)(2,1)}, /*index=5*/f32[2,256,1792]{2,0,1:T(2,128)S(1)}) fusion(f32[2,259,1792]{2,0,1:T(2,128)} %copy-done, f32[2,256]{0,1:T(8,128)S(1)} %copy.314, f32[2,256]{0,1:T(8,128)} %copy-done.28, f32[2,256]{0,1:T(8,128)} %copy-done.30, ...), kind=kLoop, calls=%fused_computation.38 | loop fusion | flops 22011136 | bytes 25730560 | tf_op jit(solution)/shard_map/transpose(jvp())/reduce_sum | solution.py:34
  379.8 6.0 %multiply_multiply_fusion.3 = (f32[2,256,1792]{2,0,1:T(2,128)S(1)}, f32[2,256,1792]{2,0,1:T(2,128)S(1)}, f32[2,256,1792]{2,0,1:T(2,128)S(1)}, f32[2,256,1792]{2,0,1:T(2,128)S(1)}) fusion(f32[2,256,1792]{2,0,1:T(2,128)S(1)} %get-tuple-element.46, f32[2,256]{0,1:T(8,128)S(1)} %copy.314, f32[1792]{0:T(1024)S(1)} %mul.599, f32[2,256]{0,1:T(8,128)S(1)} %copy-done.33, ...), kind=kLoop, calls=%fused_computation.76 | loop fusion | flops 7340032 | bytes 18386944 | tf_op jit(solution)/shard_map/transpose(jvp())/mul | solution.py:34
  385.7 6.6 %pad_add_fusion = f32[2,259,1792]{2,0,1:T(2,128)} fusion(f32[2,256,1792]{2,0,1:T(2,128)S(1)} %get-tuple-element.58, f32[2,256,1792]{2,0,1:T(2,128)S(1)} %get-tuple-element.59, f32[2,256,1792]{2,0,1:T(2,128)S(1)} %get-tuple-element.60, f32[2,256,1792]{2,0,1:T(2,128)S(1)} %get-tuple-element.57), kind=kLoop, calls=%fused_computation.29 | loop fusion | flops 2784768 | bytes 18393088 | tf_op jit(solution)/shard_map/transpose(jvp())/add_any | solution.py:35
  394.3 5.0 reduce-window.16
  410.8 4.3 copy.364
  415.1 6.6 %fusion.41 = (bf16[768]{0:T(1024)(128)(2,1)S(1)}, f32[2,256]{1,0:T(2,128)S(1)}, f32[2,256,768]{2,1,0:T(8,128)}) fusion(bf16[2,256,768]{2,1,0:T(8,128)(2,1)S(1)} %copy-done.19, f32[2,256]{1,0:T(2,128)S(1)} %copy-done.101, f32[768]{0:T(1024)S(1)} %copy-done.91, f32[2,256,768]{2,1,0:T(8,128)} %fusion.31, bf16[2,256,1816]{1,2,0:T(8,128)(2,1)} %copy.364, ...), kind=kOutput, calls=%fused_computation.96 | convolution fusion | flops 1431304960 | bytes 8589824 | tf_op jit(solution)/shard_map/dot_general | solution.py:285
  436.0 4.1 fusion.45
  443.1 24.4 %reduce-scatter.6.cloned.1.call-done = bf16[48,768]{1,0:T(8,128)(2,1)} async-done(((bf16[1536,768]{1,0:T(8,128)(2,1)}), bf16[48,768]{1,0:T(8,128)(2,1)}) %reduce-scatter.6.cloned.1.call-update) | async-done | bytes 73744 | tf_op jit(solution)/shard_map/reduce_scatter | solution.py:243
  468.4 105.7 %reduce-scatter.4.cloned.1.call-done = bf16[48,917]{1,0:T(8,128)(2,1)} async-done(((bf16[1536,917]{1,0:T(8,128)(2,1)}), bf16[48,917]{1,0:T(8,128)(2,1)}) %reduce-scatter.4.cloned.1.call-update) | async-done | bytes 88048 | tf_op jit(solution)/shard_map/reduce_scatter | solution.py:311
  (433 shorter events, 173.6 us)
Async XLA Ops:
  7.2 66.3 %all-gather.4.cloned.1.call-start = ((), (), s32[]{:S(2)}) async-start(), calls=%async_computation.3 | async-start | bytes 3041280 | tf_op jit(solution)/shard_map/all_gather | solution.py:121
  11.8 182.5 %all-gather.8.cloned.1.call-start = ((), (), s32[]{:S(2)}) async-start(), calls=%async_computation.5 | async-start | bytes 2433024 | tf_op jit(solution)/shard_map/all_gather | solution.py:128
  73.5 131.8 %all-gather.6.cloned.1.call-start = ((), (), s32[]{:S(2)}) async-start(), calls=%async_computation.4 | async-start | bytes 2433024 | tf_op jit(solution)/shard_map/all_gather | solution.py:127
  76.5 37.5 %copy-start.28 = (f32[2,256]{0,1:T(8,128)}, f32[2,256]{0,1:T(8,128)S(1)}, u32[]{:S(2)}) copy-start(f32[2,256]{0,1:T(8,128)S(1)} %copy.313) | copy-start | bytes 6148
  76.7 37.3 %copy-start.30 = (f32[2,256]{0,1:T(8,128)}, f32[2,256]{0,1:T(8,128)S(1)}, u32[]{:S(2)}) copy-start(f32[2,256]{0,1:T(8,128)S(1)} %copy.312) | copy-start | bytes 6148
  76.8 37.2 %copy-start.32 = (f32[2,256]{0,1:T(8,128)}, f32[2,256]{0,1:T(8,128)S(1)}, u32[]{:S(2)}) copy-start(f32[2,256]{0,1:T(8,128)S(1)} %copy.311) | copy-start | bytes 6148
  77.3 24.7 %copy-start.111 = (f32[2]{0:T(128)}, f32[2]{0:T(128)S(1)}, u32[]{:S(2)}) copy-start(f32[2]{0:T(128)S(1)} %slice_reduce_fusion.6) | copy-start | bytes 28
  79.4 20.2 %copy-start.109 = (f32[24]{0:T(128)}, f32[24]{0:T(128)S(1)}, u32[]{:S(2)}) copy-start(f32[24]{0:T(128)S(1)} %exponential_negate_fusion) | copy-start | bytes 292
  95.9 14.7 %collective-permute-start = (bf16[2,3,1792]{2,0,1:T(2,128)(2,1)}, bf16[2,3,1792]{2,0,1:T(2,128)(2,1)}, u32[]{:S(2)}, u32[]{:S(2)}) collective-permute-start(bf16[2,3,1792]{2,0,1:T(2,128)(2,1)} %slice.283), channel_id=1, source_target_pairs={{0,1},{1,2},{2,3},{4,5},{5,6},{6,7},{8,9},{9,10},{10,11},{12,13},{... | collective-permute-start | bytes 64520 | tf_op jit(solution)/shard_map/ppermute | solution.py:20
  110.3 331.3 %reduce-scatter.8.cloned.1.call-start = ((), (), s32[]{:S(2)}) async-start(), calls=%async_computation.8 | async-start | bytes 2433024 | tf_op jit(solution)/shard_map/reduce_scatter | solution.py:242
  130.5 56.1 %copy-start.1 = (bf16[2,256,1536]{1,2,0:T(8,128)(2,1)}, bf16[2,256,1536]{1,2,0:T(8,128)(2,1)S(1)}, u32[]{:S(2)}) copy-start(bf16[2,256,1536]{1,2,0:T(8,128)(2,1)S(1)} %copy.315) | copy-start | bytes 4718596
  130.5 21.8 %copy-start.80 = (s32[2,256]{1,0:T(2,128)S(1)}, s32[2,256]{1,0:T(2,128)}, u32[]{:S(2)}) copy-start(s32[2,256]{1,0:T(2,128)} %copy-done.79) | copy-start | bytes 6148
  132.5 10.9 %collective-permute-start.1 = (bf16[24,64,128]{2,1,0:T(8,128)(2,1)S(1)}, bf16[24,64,128]{2,1,0:T(8,128)(2,1)S(1)}, u32[]{:S(2)}, u32[]{:S(2)}) collective-permute-start(bf16[24,64,128]{2,1,0:T(8,128)(2,1)S(1)} %add_convert_fusion.7), channel_id=1, source_target_pairs={{0,1},{4,5},{8,9},{12,13},{16,17},{20,21},{24,25},{28,29}} | collective-permute-start | bytes 1179656 | tf_op jit(solution)/shard_map/ppermute | solution.py:14
  134.7 28.3 %copy-start.93 = (f32[24]{0:T(128)}, f32[24]{0:T(128)S(1)}, u32[]{:S(2)}) copy-start(f32[24]{0:T(128)S(1)} %get-tuple-element.98) | copy-start | bytes 292
  145.2 12.1 %collective-permute-start.2 = (bf16[24,64,128]{2,1,0:T(8,128)(2,1)}, bf16[24,64,128]{2,1,0:T(8,128)(2,1)}, u32[]{:S(2)}, u32[]{:S(2)}) collective-permute-start(bf16[24,64,128]{2,1,0:T(8,128)(2,1)} %get-tuple-element.76), channel_id=1, source_target_pairs={{1,2},{5,6},{9,10},{13,14},{17,18},{21,22},{25,26},{29,30}} | collective-permute-start | bytes 1179656 | tf_op jit(solution)/shard_map/ppermute | solution.py:14
  146.6 14.0 %collective-permute-start.4 = (bf16[24,64,128]{2,1,0:T(8,128)(2,1)}, bf16[24,64,128]{2,1,0:T(8,128)(2,1)}, u32[]{:S(2)}, u32[]{:S(2)}) collective-permute-start(bf16[24,64,128]{2,1,0:T(8,128)(2,1)} %get-tuple-element.77), channel_id=1, source_target_pairs={{0,1},{4,5},{8,9},{12,13},{16,17},{20,21},{24,25},{28,29}} | collective-permute-start | bytes 1179656 | tf_op jit(solution)/shard_map/ppermute | solution.py:14
  163.1 9.6 %collective-permute-start.5 = (bf16[24,64,128]{2,1,0:T(8,128)(2,1)}, bf16[24,64,128]{2,1,0:T(8,128)(2,1)}, u32[]{:S(2)}, u32[]{:S(2)}) collective-permute-start(bf16[24,64,128]{2,1,0:T(8,128)(2,1)} %get-tuple-element.75), channel_id=1, source_target_pairs={{1,2},{5,6},{9,10},{13,14},{17,18},{21,22},{25,26},{29,30}} | collective-permute-start | bytes 1179656 | tf_op jit(solution)/shard_map/ppermute | solution.py:14
  171.2 12.2 %collective-permute-start.3 = (bf16[24,64,128]{2,1,0:T(8,128)(2,1)}, bf16[24,64,128]{2,1,0:T(8,128)(2,1)}, u32[]{:S(2)}, u32[]{:S(2)}) collective-permute-start(bf16[24,64,128]{2,1,0:T(8,128)(2,1)} %get-tuple-element.74), channel_id=1, source_target_pairs={{2,3},{6,7},{10,11},{14,15},{18,19},{22,23},{26,27},{30,31}} | collective-permute-start | bytes 1179656 | tf_op jit(solution)/shard_map/ppermute | solution.py:14
  174.7 10.2 %collective-permute-start.6 = (bf16[24,64,128]{2,1,0:T(8,128)(2,1)}, bf16[24,64,128]{2,1,0:T(8,128)(2,1)}, u32[]{:S(2)}, u32[]{:S(2)}) collective-permute-start(bf16[24,64,128]{2,1,0:T(8,128)(2,1)} %add_convert_fusion.4), channel_id=1, source_target_pairs={{2,3},{6,7},{10,11},{14,15},{18,19},{22,23},{26,27},{30,31}} | collective-permute-start | bytes 1179656 | tf_op jit(solution)/shard_map/ppermute | solution.py:14
  256.5 211.0 %reduce-scatter.6.cloned.1.call-start = ((), (), s32[]{:S(2)}) async-start(), calls=%async_computation.7 | async-start | bytes 2433024 | tf_op jit(solution)/shard_map/reduce_scatter | solution.py:243
  266.0 22.6 %collective-permute-start.7 = (bf16[24,64,128]{2,1,0:T(8,128)(2,1)}, bf16[24,64,128]{2,1,0:T(8,128)(2,1)}, u32[]{:S(2)}, u32[]{:S(2)}) collective-permute-start(bf16[24,64,128]{2,1,0:T(8,128)(2,1)} %add_convert_fusion.3), channel_id=1, source_target_pairs={{3,2},{7,6},{11,10},{15,14},{19,18},{23,22},{27,26},{31,30}} | collective-permute-start | bytes 1179656 | tf_op jit(solution)/shard_map/ppermute | solution.py:14
  286.5 287.6 %reduce-scatter.4.cloned.1.call-start = ((), (), s32[]{:S(2)}) async-start(), calls=%async_computation.6 | async-start | bytes 3244032 | tf_op jit(solution)/shard_map/reduce_scatter | solution.py:311
  289.9 5.8 collective-permute-start.8
  290.6 5.1 collective-permute-start.10
  298.1 5.2 collective-permute-start.11
  302.0 27.6 %collective-permute-start.9 = (bf16[24,64,128]{2,1,0:T(8,128)(2,1)}, bf16[24,64,128]{2,1,0:T(8,128)(2,1)}, u32[]{:S(2)}, u32[]{:S(2)}) collective-permute-start(bf16[24,64,128]{2,1,0:T(8,128)(2,1)} %get-tuple-element.70), channel_id=1, source_target_pairs={{1,0},{5,4},{9,8},{13,12},{17,16},{21,20},{25,24},{29,28}} | collective-permute-start | bytes 1179656 | tf_op jit(solution)/shard_map/ppermute | solution.py:14
  304.2 39.1 %copy-start.26 = (bf16[24,64,128]{2,1,0:T(8,128)(2,1)S(1)}, bf16[24,64,128]{2,1,0:T(8,128)(2,1)}, u32[]{:S(2)}) copy-start(bf16[24,64,128]{2,1,0:T(8,128)(2,1)} %copy-done.25) | copy-start | bytes 1179652
  304.3 39.1 %collective-permute-start.12 = (bf16[24,64,128]{2,1,0:T(8,128)(2,1)}, bf16[24,64,128]{2,1,0:T(8,128)(2,1)}, u32[]{:S(2)}, u32[]{:S(2)}) collective-permute-start(bf16[24,64,128]{2,1,0:T(8,128)(2,1)} %add_convert_fusion), channel_id=1, source_target_pairs={{1,0},{5,4},{9,8},{13,12},{17,16},{21,20},{25,24},{29,28}} | collective-permute-start | bytes 1179656 | tf_op jit(solution)/shard_map/ppermute | solution.py:14
  305.9 37.5 %copy-start.41 = (bf16[24,64,128]{2,1,0:T(8,128)(2,1)S(1)}, bf16[24,64,128]{2,1,0:T(8,128)(2,1)}, u32[]{:S(2)}) copy-start(bf16[24,64,128]{2,1,0:T(8,128)(2,1)} %copy-done.40) | copy-start | bytes 1179652
  360.0 19.8 %copy-start.29 = (f32[2,256]{0,1:T(8,128)S(1)}, f32[2,256]{0,1:T(8,128)}, u32[]{:S(2)}) copy-start(f32[2,256]{0,1:T(8,128)} %copy-done.28) | copy-start | bytes 6148
  360.0 19.8 %copy-start.31 = (f32[2,256]{0,1:T(8,128)S(1)}, f32[2,256]{0,1:T(8,128)}, u32[]{:S(2)}) copy-start(f32[2,256]{0,1:T(8,128)} %copy-done.30) | copy-start | bytes 6148
  399.7 5.9 %collective-permute-start.13 = (f32[2,3,1792]{2,0,1:T(2,128)S(1)}, f32[2,3,1792]{2,0,1:T(2,128)S(1)}, u32[]{:S(2)}, u32[]{:S(2)}) collective-permute-start(f32[2,3,1792]{2,0,1:T(2,128)S(1)} %pad_add_fusion.1), channel_id=1, source_target_pairs={{1,0},{2,1},{3,2},{5,4},{6,5},{7,6},{9,8},{10,9},{11,10},{13,12},{... | collective-permute-start | bytes 129032 | tf_op jit(solution)/shard_map/ppermute | solution.py:20
  (103 other events, 638.0 us)
Sparse Core Ops, SparseCore 0:
  12.0 61.4 all-gather.3
  76.2 55.8 all-gather.7
  134.9 56.0 all-gather.5
  256.7 107.0 reduce-scatter.7
  368.9 98.6 reduce-scatter.5
  472.9 101.1 reduce-scatter.3
